TPU v7x, 512 devices: a whole 4x8x8 slice. The times are simulated.
512 devices in a mesh: dp: 4 (over y_lo), fsdp: 32 (over x, z), head: 4 (over y_hi, core).
Axes of the slice: x: 4, y: 8 (y_hi: 2, y_lo: 4; y = y_hi * 4 + y_lo), z: 8, core: 2. Of those that a mesh axis runs over, the one named last changes fastest.
Arguments:
- queries: bfloat16 [4, 8192, 2048], P('dp', 'fsdp', 'head'), may hold values from -8 to 8
- key_rows: bfloat16 [4, 8192, 2048], P('dp', 'fsdp', 'head'), may hold values from -8 to 8
- value_rows: bfloat16 [4, 8192, 2048], P('dp', 'fsdp', 'head'), may hold values from -6 to 6
- out_weight: bfloat16 [2048, 2048], P('fsdp', 'head'), may hold values from -0.125 to 0.125
- sum_lists: int32 [4, 64, 16], P('dp', 'fsdp'), may hold values from 0 to 31, as said below
- out_grad: bfloat16 [4, 8192, 2048], P('dp', 'fsdp', 'head'), may hold values from -6 to 6
Outputs:
- projected: bfloat16 [4, 8192, 2048], P('dp', 'fsdp', 'head')
- query_grad: bfloat16 [4, 8192, 2048], P('dp', 'fsdp', 'head')
- key_grad: bfloat16 [4, 8192, 2048], P('dp', 'fsdp', 'head')
- value_grad: bfloat16 [4, 8192, 2048], P('dp', 'fsdp', 'head')
- weight_grad: float32 [2048, 2048], P('fsdp', 'head')
Inputs may be any that keep to these rules, and one draw needn't show every extreme that they name: `sum_lists`: each row names 16 different strides.
All inputs are finite; a program needn't handle non-finite values.
Results may differ from a plain program's by a relative error of at most 0.028.
Values may be sent and summed in bfloat16 or wider, within the bound.
A program may use at most 64 MiB of HBM per device.

v0:
```python
from functools import reduce
import math

import jax
import jax.numpy as jnp
from jax import lax
from jax.sharding import PartitionSpec as P

HS = 128
BLK = 128
WIN = 3
STRIDE = 256
SUMC = 8


def shifted(block, axis, distance):
    devices = range(lax.axis_size(axis))
    route = [(i - distance, i) for i in devices if i - distance in devices]
    return lax.ppermute(block, axis, route)


def masked_softmax(scores, allowed):
    scores = jnp.where(allowed[:, None], scores, -jnp.inf)
    peak = jnp.max(scores, axis=3, keepdims=True)
    raised = jnp.exp(scores - peak)
    return raised / jnp.sum(raised, axis=3, keepdims=True)


def window_blocks(prior, current, blocks):
    width = current.shape[1]
    joined = jnp.concatenate([prior, current], axis=0).reshape(blocks + WIN - 1, BLK, width)
    stacked = jnp.stack([joined[offset : offset + blocks] for offset in range(WIN)], axis=1)
    return stacked.reshape(blocks, WIN * BLK, width)


def fold_window(grad_keys, blocks):
    width = grad_keys.shape[2]
    nearby = grad_keys[:, : WIN * BLK].reshape(blocks, WIN, BLK, width)
    placed = [
        jnp.pad(nearby[:, offset], ((offset, WIN - 1 - offset), (0, 0), (0, 0)))
        for offset in range(WIN)
    ]
    return reduce(jnp.add, placed).reshape((blocks + WIN - 1) * BLK, width)


def owner_rows(grad_keys, selector, fsdp_count, stride_count):
    blocks = grad_keys.shape[0]
    width = grad_keys.shape[2]
    distant = grad_keys[:, WIN * BLK :].reshape(blocks, selector.shape[1], SUMC * width)
    summed = jnp.einsum("bsn,bsc->nc", selector, distant, precision=lax.Precision.HIGHEST)
    return summed.reshape(fsdp_count, stride_count * SUMC, width)


def body(queries, key_rows, value_rows, out_weight, sum_lists, out_grad):
    query_tok = queries[0]
    key_tok = key_rows[0]
    value_tok = value_rows[0]
    grad_tok = out_grad[0]
    chosen = sum_lists[0]
    fsdp_count = lax.axis_size("fsdp")
    fsdp_pos = lax.axis_index("fsdp")
    tokens = query_tok.shape[0]
    width = query_tok.shape[1]
    head_count = width // HS
    blocks = tokens // BLK
    stride_count = tokens // STRIDE
    summary_count = stride_count * fsdp_count
    pick_count = chosen.shape[1]
    margin = (WIN - 1) * BLK
    score_scale = 1.0 / math.sqrt(HS)
    prior_keys, prior_values = shifted((key_tok, value_tok), "fsdp", 1)
    tail_keys = key_tok.reshape(stride_count, STRIDE, width)[:, STRIDE - SUMC :]
    tail_values = value_tok.reshape(stride_count, STRIDE, width)[:, STRIDE - SUMC :]
    summary_keys, summary_values = (
        lax.all_gather(tail_keys, "fsdp", axis=0, tiled=True),
        lax.all_gather(tail_values, "fsdp", axis=0, tiled=True),
    )
    far_keys = summary_keys[chosen].reshape(blocks, pick_count * SUMC, width)
    far_values = summary_values[chosen].reshape(blocks, pick_count * SUMC, width)
    block_keys = jnp.concatenate(
        [window_blocks(prior_keys, key_tok, blocks), far_keys], axis=1
    ).reshape(blocks, -1, head_count, HS)
    block_values = jnp.concatenate(
        [window_blocks(prior_values, value_tok, blocks), far_values], axis=1
    ).reshape(blocks, -1, head_count, HS)
    block_queries = query_tok.reshape(blocks, BLK, head_count, HS)
    block_ids = fsdp_pos * blocks + jnp.arange(blocks, dtype=jnp.int32)
    query_pos = block_ids[:, None] * BLK + jnp.arange(BLK, dtype=jnp.int32)[None, :]
    window_start = (block_ids - WIN + 1) * BLK
    key_pos = window_start[:, None] + jnp.arange(WIN * BLK, dtype=jnp.int32)[None, :]
    nearby_ok = (key_pos[:, None, :] >= 0) & (key_pos[:, None, :] <= query_pos[:, :, None])
    distant_ok = jnp.repeat((chosen + 1) * STRIDE <= window_start[:, None], SUMC, axis=1)
    allowed = jnp.concatenate(
        [nearby_ok, jnp.broadcast_to(distant_ok[:, None, :], (blocks, BLK, pick_count * SUMC))],
        axis=2,
    )
    scores = (
        jnp.einsum("bihd,bjhd->bhij", block_queries, block_keys, preferred_element_type=jnp.float32)
        * score_scale
    )
    weights = masked_softmax(scores, allowed)
    weights_b = weights.astype(jnp.bfloat16)
    mixed = jnp.einsum(
        "bhij,bjhd->bihd", weights_b, block_values, preferred_element_type=jnp.float32
    )
    mixed = mixed.reshape(tokens, width).astype(jnp.bfloat16)
    all_mixed = lax.all_gather(mixed, "head", axis=1, tiled=True)
    weight_cols = lax.all_gather(out_weight, "fsdp", axis=0, tiled=True)
    projected = jnp.dot(all_mixed, weight_cols, preferred_element_type=jnp.float32).astype(
        jnp.bfloat16
    )
    grad_all = lax.all_gather(grad_tok, "head", axis=1, tiled=True)
    weight_all = lax.all_to_all(weight_cols, "head", split_axis=0, concat_axis=1, tiled=True)
    grad_mixed = lax.dot_general(
        grad_all, weight_all, (((1,), (1,)), ((), ())), preferred_element_type=jnp.float32
    ).astype(jnp.bfloat16)
    grad_blocks = grad_mixed.reshape(blocks, BLK, head_count, HS)
    delta = jnp.sum(
        grad_blocks.astype(jnp.float32)
        * mixed.reshape(blocks, BLK, head_count, HS).astype(jnp.float32),
        axis=3,
    )
    delta = jnp.transpose(delta, (0, 2, 1))[:, :, :, None]
    dprob = jnp.einsum(
        "bihd,bjhd->bhij", grad_blocks, block_values, preferred_element_type=jnp.float32
    )
    dscore = (weights * (dprob - delta)).astype(jnp.bfloat16)
    query_grad = (
        jnp.einsum("bhij,bjhd->bihd", dscore, block_keys, preferred_element_type=jnp.float32)
        * score_scale
    )
    query_grad = query_grad.reshape(tokens, width).astype(jnp.bfloat16)
    key_terms = (
        jnp.einsum("bhij,bihd->bjhd", dscore, block_queries, preferred_element_type=jnp.float32)
        * score_scale
    ).reshape(blocks, -1, width)
    value_terms = jnp.einsum(
        "bhij,bihd->bjhd", weights_b, grad_blocks, preferred_element_type=jnp.float32
    ).reshape(blocks, -1, width)
    key_window = fold_window(key_terms, blocks)
    value_window = fold_window(value_terms, blocks)
    back_keys, back_values = (
        shifted(key_window[:margin].astype(jnp.bfloat16), "fsdp", -1).astype(jnp.float32),
        shifted(value_window[:margin].astype(jnp.bfloat16), "fsdp", -1).astype(jnp.float32),
    )
    selector = (
        chosen[:, :, None] == jnp.arange(summary_count, dtype=jnp.int32)[None, None, :]
    ).astype(jnp.float32)
    got_keys, got_values = (
        lax.all_to_all(
            owner_rows(key_terms, selector, fsdp_count, stride_count).astype(jnp.bfloat16),
            "fsdp",
            split_axis=0,
            concat_axis=0,
            tiled=True,
        ).astype(jnp.float32),
        lax.all_to_all(
            owner_rows(value_terms, selector, fsdp_count, stride_count).astype(jnp.bfloat16),
            "fsdp",
            split_axis=0,
            concat_axis=0,
            tiled=True,
        ).astype(jnp.float32),
    )

    def finish(window_rows, back_rows, owner_got):
        own_rows = window_rows[margin:]
        own_rows = jnp.concatenate([own_rows[: tokens - margin], own_rows + back_rows], axis=0)
        owner_sum = jnp.sum(owner_got, axis=0).reshape(stride_count, SUMC, width)
        own_rows = own_rows.reshape(stride_count, STRIDE, width)
        own_rows = jnp.concatenate(
            [own_rows[:, : STRIDE - SUMC], own_rows[:, STRIDE - SUMC :] + owner_sum], axis=1
        )
        return own_rows.reshape(tokens, width).astype(jnp.bfloat16)

    key_grad = finish(key_window, back_keys, got_keys)
    value_grad = finish(value_window, back_values, got_values)
    shard_rows = lax.psum_scatter(
        lax.dot_general(
            all_mixed, grad_tok, (((0,), (0,)), ((), ())), preferred_element_type=jnp.float32
        ).astype(jnp.bfloat16),
        "fsdp",
        scatter_dimension=0,
        tiled=True,
    )
    weight_grad = lax.psum(shard_rows, "dp").astype(jnp.float32)
    return (projected[None], query_grad[None], key_grad[None], value_grad[None], weight_grad)


def solution(mesh):
    placed = (
        P("dp", "fsdp", "head"),
        P("dp", "fsdp", "head"),
        P("dp", "fsdp", "head"),
        P("fsdp", "head"),
        P("dp", "fsdp", None),
        P("dp", "fsdp", "head"),
    )
    return jax.shard_map(
        body,
        mesh=mesh,
        in_specs=placed,
        out_specs=(
            P("dp", "fsdp", "head"),
            P("dp", "fsdp", "head"),
            P("dp", "fsdp", "head"),
            P("dp", "fsdp", "head"),
            P("fsdp", "head"),
        ),
        check_vma=False,
    )
```

profile of v0, /device:TPU:6, one launch (start us, length us, event | category | flops | bytes accessed | tf_op | source)
XLA Modules:
  0.0 558.9 jit_solution(8384365809282588198)
XLA Ops:
  8.0 0.7 all-gather.7.cloned.1.call-update
  8.7 90.5 %all-gather.7.cloned.1.call-done = bf16[2048,512]{1,0:T(8,128)(2,1)} async-done(((bf16[64,512]{1,0:T(8,128)(2,1)}), bf16[2048,512]{1,0:T(8,128)(2,1)}) %all-gather.7.cloned.1.call-update) | async-done | bytes 2097168 | tf_op jit(solution)/shard_map/all_gather | solution.py:108
  99.3 6.9 %all-to-all-start = ((bf16[4,512,512]{2,1,0:T(8,128)(2,1)}), bf16[4,512,512]{2,1,0:T(8,128)(2,1)S(1)}, u32[]{:S(2)}, u32[]{:S(2)}) async-start(bf16[4,512,512]{2,1,0:T(8,128)(2,1)} %bitcast.155), calls=%async_computation | async-start | bytes 4194304 | tf_op jit(solution)/shard_map/all_to_all | solution.py:113
  106.7 2.8 collective-permute-start
  109.6 2.7 collective-permute-start.1
  113.1 52.5 %all_gather.15 = bf16[32,8,512]{2,1,0:T(8,128)(2,1)S(1)} all-gather(bf16[1,8,512]{2,1,0:T(8,128)(2,1)S(1)} %slice.89), channel_id=1, replica_groups=mesh['dp'=4,'fsdp'=32,'head'=4] {'fsdp'}, dimensions={0}, use_global_device_ids=true | all-gather | bytes 270336 | tf_op jit(solution)/shard_map/all_gather | solution.py:76
  165.7 47.5 %all_gather.16 = bf16[32,8,512]{2,1,0:T(8,128)(2,1)S(1)} all-gather(bf16[1,8,512]{2,1,0:T(8,128)(2,1)S(1)} %slice.91), channel_id=1, replica_groups=mesh['dp'=4,'fsdp'=32,'head'=4] {'fsdp'}, dimensions={0}, use_global_device_ids=true | all-gather | bytes 270336 | tf_op jit(solution)/shard_map/all_gather | solution.py:75
  213.2 1.3 gather_fusion
  214.5 1.0 concatenate.47
  215.5 0.9 copy.104
  216.4 0.6 gather_fusion.1
  217.0 0.8 concatenate.52
  217.7 1.0 reshape_squeeze.3
  218.7 0.9 copy.122
  219.6 0.7 copy-done.11
  220.3 1.0 pad_maximum_fusion.1
  221.3 1.1 concatenate.46
  222.5 2.2 copy.103
  224.6 0.9 pad_maximum_fusion.5
  225.6 1.0 pad_maximum_fusion.2
  226.6 1.1 concatenate.51
  227.7 1.2 copy_dynamic-update-slice_fusion
  229.1 3.3 fusion.35
  232.3 2.4 copy.113
  234.7 2.7 convolution_convert_fusion.2
  237.8 1.2 multiply_reduce_fusion
  239.2 0.7 copy.169
  240.0 29.1 %all-gather.5.cloned.1.call-done = bf16[256,2048]{1,0:T(8,128)(2,1)} async-done(((bf16[256,512]{1,0:T(8,128)(2,1)}), bf16[256,2048]{1,0:T(8,128)(2,1)}) %all-gather.5.cloned.1.call-update) | async-done | bytes 1048592 | tf_op jit(solution)/shard_map/all_gather | solution.py:107
  269.1 3.3 convolution_convert_fusion
  272.4 2.1 fusion.32
  274.4 1.4 copy-done.5
  275.8 0.9 slice.133
  276.7 1.5 slice.125
  278.7 1.2 copy.154
  280.5 0.9 copy.138
  281.4 10.6 %all-to-all-start.2 = ((bf16[32,8,512]{2,1,0:T(8,128)(2,1)}), bf16[32,8,512]{2,1,0:T(8,128)(2,1)}, u32[]{:S(2)}, u32[]{:S(2)}) async-start(bf16[32,8,512]{2,1,0:T(8,128)(2,1)} %copy.138), calls=%async_computation.2 | async-start | bytes 524288 | tf_op jit(solution)/shard_map/all_to_all | solution.py:157
  292.4 0.7 slice.150
  293.1 5.2 collective-permute-start.3
  298.4 0.6 multiply_convert_fusion
  299.0 1.8 multiply_bitcast_fusion
  300.8 1.9 copy.124
  302.7 1.3 slice.116
  304.0 3.0 copy.125
  307.0 1.6 slice_bitcast_fusion.5
  309.4 1.0 slice.124
  310.4 1.2 copy.128
  311.7 0.7 slice.151
  312.5 3.3 collective-permute-start.2
  316.5 0.8 convert_element_type.115
  317.3 0.9 copy.130
  318.2 1.8 bitcast_add_fusion
  320.0 6.5 %all-to-all-start.1 = ((bf16[32,8,512]{2,1,0:T(8,128)(2,1)}), bf16[32,8,512]{2,1,0:T(8,128)(2,1)S(1)}, u32[]{:S(2)}, u32[]{:S(2)}) async-start(bf16[32,8,512]{2,1,0:T(8,128)(2,1)} %copy.130), calls=%async_computation.1 | async-start | bytes 524288 | tf_op jit(solution)/shard_map/all_to_all | solution.py:150
  326.7 1.3 slice.152
  328.1 0.7 slice.153
  328.8 1.0 convert_reduce_fusion
  329.8 0.7 fusion.20
  330.5 0.7 pad_maximum_fusion.8
  331.3 5.8 %all-to-all-done.1 = bf16[32,8,512]{2,1,0:T(8,128)(2,1)S(1)} async-done(((bf16[32,8,512]{2,1,0:T(8,128)(2,1)}), bf16[32,8,512]{2,1,0:T(8,128)(2,1)S(1)}, u32[]{:S(2)}, u32[]{:S(2)}) %all-to-all-start.1) | async-done | bytes 262176 | tf_op jit(solution)/shard_map/all_to_all | solution.py:150
  337.1 0.7 fusion.21
  337.8 1.7 pad_maximum_fusion.7
  339.5 158.1 %reduce-scatter.2.cloned.1.call-done = bf16[64,512]{1,0:T(8,128)(2,1)} async-done(((bf16[2048,512]{1,0:T(8,128)(2,1)}), bf16[64,512]{1,0:T(8,128)(2,1)}) %reduce-scatter.2.cloned.1.call-update) | async-done | bytes 65552 | tf_op jit(solution)/shard_map/reduce_scatter | solution.py:178
  497.7 1.4 fusion.6
  499.1 50.7 %all-reduce.8.cloned.1.call-done = bf16[64,512]{1,0:T(8,128)(2,1)} async-done(((bf16[64,512]{1,0:T(8,128)(2,1)}), bf16[64,512]{1,0:T(8,128)(2,1)}) %all-reduce.8.cloned.1.call-update) | async-done | bytes 65552 | tf_op jit(solution)/shard_map/psum | solution.py:186
  549.8 1.5 convert_element_type.125
  (94 shorter events, 5.4 us)
Async XLA Ops:
  8.0 91.3 %all-gather.7.cloned.1.call-start = ((), (), s32[]{:S(2)}) async-start(), calls=%async_computation.5 | async-start | bytes 2162688 | tf_op jit(solution)/shard_map/all_gather | solution.py:108
  99.3 7.5 %copy-start.8 = (bf16[1,256,512]{2,1,0:T(8,128)(2,1)S(1)}, bf16[1,256,512]{2,1,0:T(8,128)(2,1)}, u32[]{:S(2)}) copy-start(bf16[1,256,512]{2,1,0:T(8,128)(2,1)} %param.8) | copy-start | bytes 786436
  99.3 10.3 %copy-start.9 = (bf16[1,256,512]{2,1,0:T(8,128)(2,1)S(1)}, bf16[1,256,512]{2,1,0:T(8,128)(2,1)}, u32[]{:S(2)}) copy-start(bf16[1,256,512]{2,1,0:T(8,128)(2,1)} %param.7) | copy-start | bytes 786436
  99.3 13.0 %copy-start.20 = (s32[1,2,16]{2,1,0:T(2,128)S(1)}, s32[1,2,16]{2,1,0:T(2,128)}, u32[]{:S(2)}) copy-start(s32[1,2,16]{2,1,0:T(2,128)} %param.10) | copy-start | bytes 388
  99.3 133.1 %all-to-all-start = ((bf16[4,512,512]{2,1,0:T(8,128)(2,1)}), bf16[4,512,512]{2,1,0:T(8,128)(2,1)S(1)}, u32[]{:S(2)}, u32[]{:S(2)}) async-start(bf16[4,512,512]{2,1,0:T(8,128)(2,1)} %bitcast.155), calls=%async_computation | async-start | bytes 4194304 | tf_op jit(solution)/shard_map/all_to_all | solution.py:113
  106.1 128.6 %all-gather.9.cloned.1.call-start = ((), (), s32[]{:S(2)}) async-start(), calls=%async_computation.8 | async-start | bytes 1310720 | tf_op jit(solution)/shard_map/all_gather | solution.py:112
  106.7 162.4 %all-gather.5.cloned.1.call-start = ((), (), s32[]{:S(2)}) async-start(), calls=%async_computation.4 | async-start | bytes 1310720 | tf_op jit(solution)/shard_map/all_gather | solution.py:107
  106.7 112.9 %collective-permute-start = (bf16[256,512]{1,0:T(8,128)(2,1)S(1)}, bf16[256,512]{1,0:T(8,128)(2,1)S(1)}, u32[]{:S(2)}, u32[]{:S(2)}) collective-permute-start(bf16[256,512]{1,0:T(8,128)(2,1)S(1)} %bitcast.163), channel_id=1, source_target_pairs={{0,4},{4,8},{8,12},{12,16},{16,20},{20,24},{24,28},{28,32},{32,36}... | collective-permute-start | bytes 786440 | tf_op jit(solution)/shard_map/ppermute | solution.py:19
  109.6 115.1 %collective-permute-start.1 = (bf16[256,512]{1,0:T(8,128)(2,1)S(1)}, bf16[256,512]{1,0:T(8,128)(2,1)}, u32[]{:S(2)}, u32[]{:S(2)}) collective-permute-start(bf16[256,512]{1,0:T(8,128)(2,1)S(1)} %bitcast.166), channel_id=1, source_target_pairs={{0,4},{4,8},{8,12},{12,16},{16,20},{20,24},{24,28},{28,32},{32,36}... | collective-permute-start | bytes 786440 | tf_op jit(solution)/shard_map/ppermute | solution.py:19
  219.6 0.7 copy-start.11
  226.6 2.4 copy-start.12
  229.1 43.3 %copy-start.1 = (bf16[2,512,4,128]{3,1,2,0:T(8,128)(2,1)}, bf16[2,512,4,128]{3,1,2,0:T(8,128)(2,1)S(1)}, u32[]{:S(2)}) copy-start(bf16[2,512,4,128]{3,1,2,0:T(8,128)(2,1)S(1)} %copy_dynamic-update-slice_fusion.1) | copy-start | bytes 3145732
  234.7 3.0 copy-start.13
  234.7 3.0 copy-start.14
  234.7 3.0 copy-start.16
  237.7 1.3 copy-start.18
  237.7 31.3 %copy-start.10 = (bf16[1,256,512]{2,1,0:T(8,128)(2,1)S(1)}, bf16[1,256,512]{2,1,0:T(8,128)(2,1)}, u32[]{:S(2)}) copy-start(bf16[1,256,512]{2,1,0:T(8,128)(2,1)} %param.11) | copy-start | bytes 786436
  239.9 257.7 %reduce-scatter.2.cloned.1.call-start = ((), (), s32[]{:S(2)}) async-start(), calls=%async_computation.6 | async-start | bytes 2162688 | tf_op jit(solution)/shard_map/reduce_scatter | solution.py:178
  274.4 1.4 copy-start.5
  281.4 38.6 %all-to-all-start.2 = ((bf16[32,8,512]{2,1,0:T(8,128)(2,1)}), bf16[32,8,512]{2,1,0:T(8,128)(2,1)}, u32[]{:S(2)}, u32[]{:S(2)}) async-start(bf16[32,8,512]{2,1,0:T(8,128)(2,1)} %copy.138), calls=%async_computation.2 | async-start | bytes 524288 | tf_op jit(solution)/shard_map/all_to_all | solution.py:157
  292.0 6.3 %copy-start.21 = (f32[2,4,128,512]{2,3,1,0:T(8,128)S(1)}, f32[2,4,128,512]{2,3,1,0:T(8,128)}, u32[]{:S(2)}) copy-start(f32[2,4,128,512]{2,3,1,0:T(8,128)} %get-tuple-element.12) | copy-start | bytes 6291460
  292.2 6.1 %copy-start.15 = (bf16[2,384,4,128]{1,3,2,0:T(8,128)(2,1)S(1)}, bf16[2,384,4,128]{1,3,2,0:T(8,128)(2,1)}, u32[]{:S(2)}) copy-start(bf16[2,384,4,128]{1,3,2,0:T(8,128)(2,1)} %copy.103) | copy-start | bytes 2359300
  292.2 6.1 %copy-start.17 = (bf16[2,128,4,128]{1,3,2,0:T(8,128)(2,1)S(1)}, bf16[2,128,4,128]{1,3,2,0:T(8,128)(2,1)}, u32[]{:S(2)}) copy-start(bf16[2,128,4,128]{1,3,2,0:T(8,128)(2,1)} %copy.104) | copy-start | bytes 786436
  292.2 6.1 %copy-start.19 = (bf16[2,128,4,128]{1,3,2,0:T(8,128)(2,1)S(1)}, bf16[2,128,4,128]{1,3,2,0:T(8,128)(2,1)}, u32[]{:S(2)}) copy-start(bf16[2,128,4,128]{1,3,2,0:T(8,128)(2,1)} %copy-done.18) | copy-start | bytes 786436
  292.4 5.9 %copy-start.3 = (f32[4,128,512]{2,1,0:T(8,128)}, f32[4,128,512]{2,1,0:T(8,128)S(1)}, u32[]{:S(2)}) copy-start(f32[4,128,512]{2,1,0:T(8,128)S(1)} %pad_add_fusion) | copy-start | bytes 3145732
  293.1 25.1 %collective-permute-start.3 = (bf16[256,512]{1,0:T(8,128)(2,1)}, bf16[256,512]{1,0:T(8,128)(2,1)}, u32[]{:S(2)}, u32[]{:S(2)}) collective-permute-start(bf16[256,512]{1,0:T(8,128)(2,1)} %bitcast.46), channel_id=1, source_target_pairs={{4,0},{8,4},{12,8},{16,12},{20,16},{24,20},{28,24},{32,28},{36,32}... | collective-permute-start | bytes 786440 | tf_op jit(solution)/shard_map/ppermute | solution.py:19
  307.0 1.7 copy-start.2
  309.4 6.9 %copy-start.4 = (f32[4,128,512]{2,1,0:T(8,128)}, f32[4,128,512]{2,1,0:T(8,128)S(1)}, u32[]{:S(2)}) copy-start(f32[4,128,512]{2,1,0:T(8,128)S(1)} %pad_add_fusion.1) | copy-start | bytes 3145732
  312.5 14.2 %collective-permute-start.2 = (bf16[256,512]{1,0:T(8,128)(2,1)}, bf16[256,512]{1,0:T(8,128)(2,1)S(1)}, u32[]{:S(2)}, u32[]{:S(2)}) collective-permute-start(bf16[256,512]{1,0:T(8,128)(2,1)} %bitcast.32), channel_id=1, source_target_pairs={{4,0},{8,4},{12,8},{16,12},{20,16},{24,20},{28,24},{32,28},{36,32}... | collective-permute-start | bytes 786440 | tf_op jit(solution)/shard_map/ppermute | solution.py:19
  315.8 2.4 slice-start
  316.3 10.3 %slice-start.1 = ((f32[4,128,512]{2,1,0:T(8,128)}), f32[2,128,512]{2,1,0:T(8,128)S(1)}, s32[]{:S(2)}) async-start(f32[4,128,512]{2,1,0:T(8,128)} %copy-done.4), calls=%async_computation.10 | async-start | bytes 1048576 | tf_op jit(solution)/shard_map/slice | solution.py:167
  320.0 17.0 %all-to-all-start.1 = ((bf16[32,8,512]{2,1,0:T(8,128)(2,1)}), bf16[32,8,512]{2,1,0:T(8,128)(2,1)S(1)}, u32[]{:S(2)}, u32[]{:S(2)}) async-start(bf16[32,8,512]{2,1,0:T(8,128)(2,1)} %copy.130), calls=%async_computation.1 | async-start | bytes 524288 | tf_op jit(solution)/shard_map/all_to_all | solution.py:150
  326.6 171.1 %copy-start = (bf16[256,2048]{1,0:T(8,128)(2,1)S(1)}, bf16[256,2048]{1,0:T(8,128)(2,1)}, u32[]{:S(2)}) copy-start(bf16[256,2048]{1,0:T(8,128)(2,1)} %all-gather.5.cloned.1.call-done) | copy-start | bytes 3145732
  326.6 223.2 %all-reduce.8.cloned.1.call-start = ((), (), s32[]{:S(2)}) async-start(), calls=%async_computation.7 | async-start | bytes 131072 | tf_op jit(solution)/shard_map/psum | solution.py:186
  326.7 1.4 copy-start.7
  326.7 171.0 %copy-start.6 = (bf16[2048,512]{1,0:T(8,128)(2,1)S(1)}, bf16[2048,512]{1,0:T(8,128)(2,1)}, u32[]{:S(2)}) copy-start(bf16[2048,512]{1,0:T(8,128)(2,1)} %all-gather.7.cloned.1.call-done) | copy-start | bytes 6291460
Sparse Core Ops, SparseCore 0:
  12.0 87.2 all-gather.6
  272.5 225.1 reduce-scatter.1
Sparse Core Ops, SparseCore 1:
  108.7 40.2 all-gather.8
  240.0 29.0 all-gather.4
  497.7 52.0 all-reduce.7
where the time goes:
time: 560 us; the launch traced here: 559 us
  waiting for transfers between devices  336 us (60%)
  blocking collectives  100 us (18%)
  local copies, waits for them, and re-layouts  39 us (7%)
  starting transfers between devices  38.1 us (7%)
  matrix products  17.8 us (3%)
  between operations  16.3 us (3%)
  other arithmetic  12.2 us (2%)
    reduce_scatter x1, waiting for transfers between devices, body(): lax.psum_scatter(lax.dot_general(all_mixed, grad_tok, (((0,), (0,)), ((),...  158 us
    all_gather x1, waiting for transfers between devices, body(): weight_cols = lax.all_gather(out_weight, 'fsdp', axis=0, tiled=True)  90.5 us
    all_gather x1, blocking collectives, body(): lax.all_gather(tail_values, 'fsdp', axis=0, tiled=True)  52.5 us
    psum x1, waiting for transfers between devices, body(): weight_grad = lax.psum(shard_rows, 'dp').astype(jnp.float32)  50.7 us
    all_gather x1, blocking collectives, body(): lax.all_gather(tail_keys, 'fsdp', axis=0, tiled=True)  47.5 us
    all_gather x1, waiting for transfers between devices, body(): all_mixed = lax.all_gather(mixed, 'head', axis=1, tiled=True)  29.1 us
    ppermute x4, starting transfers between devices, shifted(): return lax.ppermute(block, axis, route)  14 us
  transfers between devices with their start and end apart: 12, of which 5 were waited for; matrix products, arithmetic and copies ran while one was open for 10% of the time, Pallas kernels for 0%

commit v1 on v0

v1 whole, which is shorter than its diff:
```python
import math

import jax
import jax.numpy as jnp
from jax import lax
from jax.experimental import pallas as pl
from jax.experimental.pallas import tpu as pltpu
from jax.sharding import PartitionSpec as P

HS = 128
BLK = 128
STRIDE = 256
SUMC = 8
NX = 4
NZ = 8
NH = 4
ND = 4
TOK = 256
WID = 512
ROWS = 64
HALF = ROWS // 2
HEADS = WID // HS
FSDP = NX * NZ
SCALE = 1.0 / math.sqrt(HS)
NEG = -1e30
MESH = pl.DeviceIdType.MESH
BF = jnp.bfloat16
F32 = jnp.float32


def place():
    d = lax.axis_index("dp")
    f = lax.axis_index("fsdp")
    h = lax.axis_index("head")
    return d, lax.div(f, NZ), lax.rem(f, NZ), h


def send(src, dst, ssem, rsem, dev):
    return pltpu.make_async_remote_copy(
        src_ref=src, dst_ref=dst, send_sem=ssem, recv_sem=rsem, device_id=dev, device_id_type=MESH
    )


def meet(bar, count, swapped):
    @pl.when(swapped)
    def _():
        pl.semaphore_wait(bar, count + 1)

    @pl.when(jnp.logical_not(swapped))
    def _():
        pl.semaphore_wait(bar, count)


class Links:
    def __init__(self):
        self.d, self.x, self.z, self.h = place()
        d, x, z, h = self.d, self.x, self.z, self.h
        self.xr, self.xl = lax.rem(x + 1, NX), lax.rem(x + NX - 1, NX)
        self.xo = lax.rem(x + 2, NX)
        self.zr, self.zl = lax.rem(z + 1, NZ), lax.rem(z + NZ - 1, NZ)
        f = x * NZ + z
        self.f = f
        self.sib = h + 1 - 2 * lax.rem(h, 2)
        self.rem = lax.rem(h + 2, NH)
        self.far = lax.rem(self.sib + 2, NH)
        self.dev_xr = (d, self.xr * NZ + z, h)
        self.dev_xl = (d, self.xl * NZ + z, h)
        self.dev_zr = (d, x * NZ + self.zr, h)
        self.dev_zl = (d, x * NZ + self.zl, h)
        self.dev_next = (d, lax.rem(f + 1, FSDP), h)
        self.dev_prev = (d, lax.rem(f + FSDP - 1, FSDP), h)
        self.dev_sib = (d, f, self.sib)
        self.dev_rem = (d, f, self.rem)
        self.dev_swap = (d, h * NZ + z, x)
        self.zs = [lax.rem(z + i, NZ) for i in range(NZ)]
        self.xs = [lax.rem(x + i, NX) for i in range(NX)]

    def dev_z(self, i):
        return (self.d, self.x * NZ + self.zs[i], self.h)

    def dev_x(self, i):
        return (self.d, self.xs[i] * NZ + self.z, self.h)


def gather_kernel(
    w_ref, g_ref, k_ref, v_ref, t_ref,
    wf, ga, pk, pv, sa,
    swap_sem, loc_sem, zr_s, zr_r, zl_s, zl_r, xr_s, xr_r, xl_s, xl_r, fr_s, fr_r, fl_s, fl_r,
    kv_s, kv_r, g_s, g_r, sz_s, sz_r, sx_s, sx_r,
):
    m = Links()
    d, x, z, h = m.d, m.x, m.z, m.h
    bar = pltpu.get_barrier_semaphore()

    def hello(dev):
        pl.semaphore_signal(bar, inc=1, device_id=dev, device_id_type=MESH)

    for i in range(1, NZ):
        hello(m.dev_z(i))
    for i in range(1, NX):
        hello(m.dev_x(i))
    hello(m.dev_sib)
    hello(m.dev_rem)
    hello(m.dev_next)
    hello(m.dev_prev)
    swapped = x != h

    @pl.when(swapped)
    def _():
        hello(m.dev_swap)

    meet(bar, (NZ - 1) + (NX - 1) + 4, swapped)

    @pl.when(swapped)
    def _():
        send(w_ref, wf.at[h, z], swap_sem.at[0], swap_sem.at[1], m.dev_swap).start()

    @pl.when(jnp.logical_not(swapped))
    def _():
        pltpu.make_async_copy(w_ref, wf.at[x, z], loc_sem.at[0]).start()

    own_t = pltpu.make_async_copy(t_ref, sa.at[x, z], loc_sem.at[1])
    own_t.start()
    tz = [send(t_ref, sa.at[x, z], sz_s.at[i - 1], sz_r.at[i - 1], m.dev_z(i)) for i in range(1, NZ)]
    for c in tz:
        c.start()
    own_g = pltpu.make_async_copy(g_ref, ga.at[h], loc_sem.at[2])
    own_g.start()
    g_rem = send(g_ref, ga.at[h], g_s.at[0], g_r.at[0], m.dev_rem)
    g_rem.start()
    g_sib = send(g_ref, ga.at[h], g_s.at[1], g_r.at[1], m.dev_sib)
    g_sib.start()
    ks = send(k_ref, pk, kv_s.at[0], kv_r.at[0], m.dev_next)
    ks.start()
    vs = send(v_ref, pv, kv_s.at[1], kv_r.at[1], m.dev_next)
    vs.start()

    @pl.when(swapped)
    def _():
        send(w_ref, wf.at[h, z], swap_sem.at[0], swap_sem.at[1], m.dev_swap).wait()

    @pl.when(jnp.logical_not(swapped))
    def _():
        pltpu.make_async_copy(w_ref, wf.at[x, z], loc_sem.at[0]).wait()

    pending = [own_t, own_g, g_sib]
    sends = list(tz) + [g_rem, ks, vs]

    order = [("own", 0), ("r", 1), ("l", 1), ("r", 2), ("l", 2), ("r", 3), ("l", 3), ("r", 4)]
    where = []
    for kind, s in order:
        where.append(z if kind == "own" else m.zs[(NZ - s) % NZ] if kind == "r" else m.zs[s])

    def zright(s):
        slot = wf.at[x, m.zs[(NZ - s) % NZ]]
        return send(slot, slot, zr_s.at[s], zr_r.at[s], m.dev_zr)

    def zleft(s):
        slot = wf.at[x, m.zs[s]]
        return send(slot, slot, zl_s.at[s], zl_r.at[s], m.dev_zl)

    def xsend(n):
        slot = wf.at[x, where[n]]
        return (
            send(slot, slot, xr_s.at[n], xr_r.at[n], m.dev_xr),
            send(slot, slot, xl_s.at[n], xl_r.at[n], m.dev_xl),
        )

    def xforward(n):
        a = wf.at[m.xl, where[n], pl.ds(0, HALF)]
        b = wf.at[m.xr, where[n], pl.ds(HALF, HALF)]
        return (
            send(a, a, fr_s.at[n], fr_r.at[n], m.dev_xr),
            send(b, b, fl_s.at[n], fl_r.at[n], m.dev_xl),
        )

    zrs = {}
    zls = {}
    xsd = {}
    xfd = {}

    def forward(n):
        xsd[n][0].wait_recv()
        xfd[n] = xforward(n)
        xfd[n][0].start()
        xsd[n][1].wait_recv()
        xfd[n][1].start()

    g_rem_pass = send(ga.at[m.rem], ga.at[m.rem], g_s.at[2], g_r.at[2], m.dev_sib)
    xsum = []
    for n, (kind, s) in enumerate(order):
        if kind == "own":
            zrs[0], zls[0] = zright(0), zleft(0)
            zrs[0].start()
            zls[0].start()
        elif kind == "r":
            zrs[s - 1].wait_recv()
            if s < 4:
                zrs[s] = zright(s)
                zrs[s].start()
        else:
            zls[s - 1].wait_recv()
            if s < 3:
                zls[s] = zleft(s)
                zls[s].start()
        xsd[n] = xsend(n)
        xsd[n][0].start()
        xsd[n][1].start()
        if n == 2:
            own_t.wait()
            for c in tz:
                c.wait_recv()
            slab = sa.at[x]
            for i in range(1, NX):
                c = send(slab, slab, sx_s.at[i - 1], sx_r.at[i - 1], m.dev_x(i))
                c.start()
                xsum.append(c)
        if n >= 2:
            forward(n - 2)
    forward(NZ - 2)
    g_rem.wait_recv()
    g_rem_pass.start()
    forward(NZ - 1)
    for n in range(NZ):
        xfd[n][0].wait_recv()
        xfd[n][1].wait_recv()
    own_g.wait()
    ks.wait_recv()
    vs.wait_recv()
    g_sib.wait_recv()
    g_rem_pass.wait_recv()
    for c in xsum:
        c.wait_recv()
    for c in tz + [g_rem, g_sib, g_rem_pass, ks, vs] + xsum:
        c.wait_send()
    for c in list(zrs.values()) + list(zls.values()):
        c.wait_send()
    for n in range(NZ):
        for c in (*xsd[n], *xfd[n]):
            c.wait_send()


def vmem(n):
    return [pl.BlockSpec(memory_space=pltpu.VMEM)] * n


def gather_inputs(w, g, k, v, t):
    dma = pltpu.SemaphoreType.DMA
    return pl.pallas_call(
        gather_kernel,
        name="gather_inputs",
        out_shape=(
            jax.ShapeDtypeStruct((NX, NZ, ROWS, WID), BF),
            jax.ShapeDtypeStruct((NH, TOK, WID), BF),
            jax.ShapeDtypeStruct((TOK, WID), BF),
            jax.ShapeDtypeStruct((TOK, WID), BF),
            jax.ShapeDtypeStruct((NX, NZ, 2, SUMC, WID), BF),
        ),
        in_specs=vmem(5),
        out_specs=tuple(vmem(5)),
        scratch_shapes=[dma((2,)), dma((3,))]
        + [dma((4,)), dma((4,)), dma((3,)), dma((3,))]
        + [dma((NZ,))] * 8
        + [dma((2,)), dma((2,)), dma((3,)), dma((3,))]
        + [dma((NZ - 1,)), dma((NZ - 1,)), dma((NX - 1,)), dma((NX - 1,))],
        compiler_params=pltpu.CompilerParams(
            collective_id=0, has_side_effects=True, vmem_limit_bytes=20 << 20
        ),
    )(w, g, k, v, t)


def dot_nt(a, b):
    return lax.dot_general(a, b, (((1,), (1,)), ((), ())), preferred_element_type=F32)


def dot_tn(a, b):
    return lax.dot_general(a, b, (((0,), (0,)), ((), ())), preferred_element_type=F32)


def dot_nn(a, b):
    return lax.dot_general(a, b, (((1,), (0,)), ((), ())), preferred_element_type=F32)


def attend_kernel(
    q_ref, k_ref, v_ref, pk, pv, sa, wf, ga, bias_ref,
    pp, pw, dq, dko, dvo, dkb, dvb, ds,
    gm_s, mx_s, sk_s, sv_s,
):
    first = lax.axis_index("fsdp") == 0
    sk_s[...] = sa[:, :, 0].astype(F32).reshape(TOK, WID).astype(BF)
    sv_s[...] = sa[:, :, 1].astype(F32).reshape(TOK, WID).astype(BF)
    gm = dot_nt(ga[0], wf[0].reshape(WID, WID))
    for c in range(1, NX):
        gm += dot_nt(ga[c], wf[c].reshape(WID, WID))
    gm_s[...] = gm.astype(BF)
    key_at = lax.broadcasted_iota(jnp.int32, (TOK, TOK), 0)
    query_at = lax.broadcasted_iota(jnp.int32, (TOK, TOK), 1)
    own_bias = jnp.where(key_at <= query_at, 0.0, NEG)
    low = jnp.where(query_at < BLK, 0, BLK) + jnp.where(first, 2 * TOK, 0)
    prior_bias = jnp.where(key_at >= low, 0.0, NEG)
    far_bias = bias_ref[...]
    for n in range(HEADS):
        cols = pl.ds(n * HS, HS)
        q = q_ref[:, cols]
        keys = (pk[:, cols], k_ref[:, cols], sk_s[:, cols])
        values = (pv[:, cols], v_ref[:, cols], sv_s[:, cols])
        scores = [
            dot_nt(key, q) * SCALE + bias
            for key, bias in zip(keys, (prior_bias, own_bias, far_bias))
        ]
        peak = jnp.max(jnp.maximum(jnp.maximum(scores[0], scores[1]), scores[2]), axis=0, keepdims=True)
        raised = [jnp.exp(s - peak) for s in scores]
        total = jnp.sum(raised[0] + raised[1] + raised[2], axis=0, keepdims=True)
        scale = 1.0 / total
        weights = [e * scale for e in raised]
        weights_b = [e.astype(BF) for e in weights]
        mixed_t = dot_tn(values[0], weights_b[0])
        for value, e in zip(values[1:], weights_b[1:]):
            mixed_t += dot_tn(value, e)
        mixed_tb = mixed_t.astype(BF)
        mx_s[:, cols] = mixed_t.T.astype(BF)
        for c in range(NH):
            part = dot_nn(mixed_tb, ga[c]).astype(BF)
            pw[c, pl.ds(2 * n, 2)] = part.reshape(2, ROWS, WID)
        grad = gm_s[:, cols]
        delta = jnp.sum(grad.astype(F32).T * mixed_tb.astype(F32), axis=0, keepdims=True)
        dscore = [
            (e * (dot_nt(value, grad) - delta)).astype(BF) for e, value in zip(weights, values)
        ]
        dq_t = dot_tn(keys[0], dscore[0])
        for key, e in zip(keys[1:], dscore[1:]):
            dq_t += dot_tn(key, e)
        dq[:, cols] = (dq_t.T * SCALE).astype(BF)
        dkb[:, cols] = (dot_nn(dscore[0], q) * SCALE).astype(BF)
        dko[:, cols] = dot_nn(dscore[1], q) * SCALE
        far_k = dot_nn(dscore[2], q) * SCALE
        ds[:, :, 0, :, cols] = far_k.reshape(NX, NZ, SUMC, HS).astype(BF)
        dvb[:, cols] = dot_nn(weights_b[0], grad).astype(BF)
        dvo[:, cols] = dot_nn(weights_b[1], grad)
        far_v = dot_nn(weights_b[2], grad)
        ds[:, :, 1, :, cols] = far_v.reshape(NX, NZ, SUMC, HS).astype(BF)
    for c in range(NH):
        pp[c] = dot_nn(mx_s[...], wf[c].reshape(WID, WID)).astype(BF)


def attend(q, k, v, pk, pv, sa, wf, ga, bias):
    return pl.pallas_call(
        attend_kernel,
        name="attend",
        out_shape=(
            jax.ShapeDtypeStruct((NH, TOK, WID), BF),
            jax.ShapeDtypeStruct((NH, NZ, ROWS, WID), BF),
            jax.ShapeDtypeStruct((TOK, WID), BF),
            jax.ShapeDtypeStruct((TOK, WID), F32),
            jax.ShapeDtypeStruct((TOK, WID), F32),
            jax.ShapeDtypeStruct((TOK, WID), BF),
            jax.ShapeDtypeStruct((TOK, WID), BF),
            jax.ShapeDtypeStruct((NX, NZ, 2, SUMC, WID), BF),
        ),
        in_specs=vmem(9),
        out_specs=tuple(vmem(8)),
        scratch_shapes=[pltpu.VMEM((TOK, WID), BF)] * 4,
        compiler_params=pltpu.CompilerParams(vmem_limit_bytes=30 << 20),
    )(q, k, v, pk, pv, sa, wf, ga, bias)


def reduce_kernel(
    pp, pw, dko, dvo, dkb, dvb, ds,
    proj, kg, vg, wg,
    arm, xrm, back, pin, bx, zin, zout, fin, fout, sx, szo, szi,
    a_s, a_r, b_s, b_r, z_s, z_r, f_s, f_r, loc_sem, bk_s, bk_r, p_s, p_r, sx_s, sx_r, sz_s, sz_r,
):
    m = Links()
    d, x, z, h = m.d, m.x, m.z, m.h
    bar = pltpu.get_barrier_semaphore()

    def hello(dev):
        pl.semaphore_signal(bar, inc=1, device_id=dev, device_id_type=MESH)

    def owner(i):
        return (lax.rem(d + i, ND), h * NZ + z, x)

    for i in range(1, NZ):
        hello(m.dev_z(i))
    for i in range(1, NX):
        hello(m.dev_x(i))
    hello(m.dev_sib)
    hello(m.dev_rem)
    hello(m.dev_next)
    hello(m.dev_prev)
    for i in range(1, ND):
        hello(owner(i))
    swapped = x != h

    @pl.when(swapped)
    def _():
        hello(owner(0))

    meet(bar, (NZ - 1) + (NX - 1) + 4 + (ND - 1), swapped)

    rows = [m.zs[(i + 1) % NZ] for i in range(NZ)]

    def leg_a(n):
        r = rows[n]
        return (
            send(pw.at[m.xo, r, pl.ds(0, HALF)], arm.at[0, n], a_s.at[0, n], a_r.at[0, n], m.dev_xr),
            send(pw.at[m.xo, r, pl.ds(HALF, HALF)], arm.at[1, n], a_s.at[1, n], a_r.at[1, n], m.dev_xl),
        )

    a_legs = [leg_a(n) for n in range(NZ)]
    for n in range(NZ):
        a_legs[n][0].start()
        a_legs[n][1].start()
    s_legs = [
        send(ds.at[m.xs[i]], sx.at[i - 1], sx_s.at[i - 1], sx_r.at[i - 1], m.dev_x(i)) for i in range(1, NX)
    ]
    for c in s_legs:
        c.start()
    bk = (
        send(dkb, back.at[0], bk_s.at[0], bk_r.at[0], m.dev_prev),
        send(dvb, back.at[1], bk_s.at[1], bk_r.at[1], m.dev_prev),
    )
    p_legs = [
        send(pp.at[m.far], pin.at[0], p_s.at[0], p_r.at[0], m.dev_sib),
        send(pp.at[m.sib], pin.at[1], p_s.at[1], p_r.at[1], m.dev_sib),
    ]
    p_legs[0].start()
    p_legs[1].start()
    bk[0].start()
    bk[1].start()
    p_legs[0].wait_recv()
    pin[3] = (pin[0].astype(F32) + pp[m.rem].astype(F32)).astype(BF)

    def leg_b(n):
        return (
            send(bx.at[0, n], xrm.at[0, n], b_s.at[0, n], b_r.at[0, n], m.dev_xr),
            send(bx.at[1, n], xrm.at[1, n], b_s.at[1, n], b_r.at[1, n], m.dev_xl),
        )

    b_legs = {}
    z_legs = {}

    def stage_b(n):
        r = rows[n]
        a_legs[n][0].wait_recv()
        bx[0, n, pl.ds(0, HALF)] = (
            arm[0, n].astype(F32) + pw[m.xr, r, pl.ds(0, HALF)].astype(F32)
        ).astype(BF)
        bx[0, n, pl.ds(HALF, HALF)] = pw[m.xr, r, pl.ds(HALF, HALF)]
        a_legs[n][1].wait_recv()
        bx[1, n, pl.ds(0, HALF)] = pw[m.xl, r, pl.ds(0, HALF)]
        bx[1, n, pl.ds(HALF, HALF)] = (
            arm[1, n].astype(F32) + pw[m.xl, r, pl.ds(HALF, HALF)].astype(F32)
        ).astype(BF)
        b_legs[n] = leg_b(n)
        b_legs[n][0].start()
        b_legs[n][1].start()

    def stage_z(n):
        b_legs[n][0].wait_recv()
        b_legs[n][1].wait_recv()
        zout[n] = (
            xrm[0, n].astype(F32) + xrm[1, n].astype(F32) + pw[x, rows[n]].astype(F32)
        ).astype(BF)
        if n < NZ - 1:
            z_legs[n] = send(zout.at[n], zin.at[n], z_s.at[n], z_r.at[n], m.dev_z(n + 1))
            z_legs[n].start()

    stage_b(0)
    p_legs.append(send(pin.at[3], pin.at[2], p_s.at[2], p_r.at[2], m.dev_rem))
    p_legs[2].start()
    stage_b(1)
    for c in s_legs:
        c.wait_recv()
    szo[...] = (
        (ds[x].astype(F32) + sx[0].astype(F32)) + (sx[1].astype(F32) + sx[2].astype(F32))
    ).astype(BF)
    t_legs = [
        send(szo.at[m.zs[i]], szi.at[i - 1], sz_s.at[i - 1], sz_r.at[i - 1], m.dev_z(i)) for i in range(1, NZ)
    ]
    for c in t_legs:
        c.start()
    for n in range(2, NZ):
        stage_b(n)
        stage_z(n - 2)
    stage_z(NZ - 2)
    stage_z(NZ - 1)
    total = zout[NZ - 1].astype(F32)
    for n in range(NZ - 1):
        z_legs[n].wait_recv()
        total += zin[n].astype(F32)
    fout[...] = total.astype(BF)
    f_legs = [send(fout, fin.at[i], f_s.at[i], f_r.at[i], owner(i)) for i in range(ND)]
    for i in range(1, ND):
        f_legs[i].start()

    @pl.when(swapped)
    def _():
        f_legs[0].start()

    @pl.when(jnp.logical_not(swapped))
    def _():
        pltpu.make_async_copy(fout, fin.at[0], loc_sem).start()

    p_legs[1].wait_recv()
    p_legs[2].wait_recv()
    proj[...] = (pp[h].astype(F32) + pin[1].astype(F32) + pin[2].astype(F32)).astype(BF)
    own = szo[z].astype(F32)
    for i in range(NZ - 1):
        t_legs[i].wait_recv()
        own += szi[i].astype(F32)
    keep = jnp.where(m.f == FSDP - 1, 0.0, 1.0)
    for j, (out, mine) in enumerate(((kg, dko), (vg, dvo))):
        bk[j].wait_recv()
        out[pl.ds(0, TOK - 16)] = (
            mine[pl.ds(0, TOK - 16)] + back[j, pl.ds(0, TOK - 16)].astype(F32) * keep
        ).astype(BF)
        tail = mine[pl.ds(TOK - 16, 16)] + back[j, pl.ds(TOK - 16, 16)].astype(F32) * keep
        tail += jnp.concatenate([jnp.zeros((8, WID), F32), own[j]], axis=0)
        out[pl.ds(TOK - 16, 16)] = tail.astype(BF)

    for i in range(1, ND):
        f_legs[i].wait_recv()

    @pl.when(swapped)
    def _():
        f_legs[0].wait()

    @pl.when(jnp.logical_not(swapped))
    def _():
        pltpu.make_async_copy(fout, fin.at[0], loc_sem).wait()

    wg[...] = (fin[0].astype(F32) + fin[1].astype(F32)) + (fin[2].astype(F32) + fin[3].astype(F32))
    for c in s_legs + list(bk) + p_legs + t_legs + f_legs[1:]:
        c.wait_send()
    for n in range(NZ):
        for c in (*a_legs[n], *b_legs[n]):
            c.wait_send()
    for c in z_legs.values():
        c.wait_send()


def reduce_gradients(pp, pw, dko, dvo, dkb, dvb, ds):
    dma = pltpu.SemaphoreType.DMA
    return pl.pallas_call(
        reduce_kernel,
        name="reduce_gradients",
        out_shape=(
            jax.ShapeDtypeStruct((TOK, WID), BF),
            jax.ShapeDtypeStruct((TOK, WID), BF),
            jax.ShapeDtypeStruct((TOK, WID), BF),
            jax.ShapeDtypeStruct((ROWS, WID), F32),
        ),
        in_specs=vmem(7),
        out_specs=tuple(vmem(4)),
        scratch_shapes=[
            pltpu.VMEM((2, NZ, HALF, WID), BF),
            pltpu.VMEM((2, NZ, ROWS, WID), BF),
            pltpu.VMEM((2, TOK, WID), BF),
            pltpu.VMEM((4, TOK, WID), BF),
            pltpu.VMEM((2, NZ, ROWS, WID), BF),
            pltpu.VMEM((NZ - 1, ROWS, WID), BF),
            pltpu.VMEM((NZ, ROWS, WID), BF),
            pltpu.VMEM((ND, ROWS, WID), BF),
            pltpu.VMEM((ROWS, WID), BF),
            pltpu.VMEM((NX - 1, NZ, 2, SUMC, WID), BF),
            pltpu.VMEM((NZ, 2, SUMC, WID), BF),
            pltpu.VMEM((NZ - 1, 2, SUMC, WID), BF),
        ]
        + [dma((2, NZ))] * 4
        + [dma((NZ - 1,)), dma((NZ - 1,)), dma((ND,)), dma((ND,)), dma]
        + [dma((2,)), dma((2,)), dma((3,)), dma((3,))]
        + [dma((NX - 1,)), dma((NX - 1,)), dma((NZ - 1,)), dma((NZ - 1,))],
        compiler_params=pltpu.CompilerParams(
            collective_id=1, has_side_effects=True, vmem_limit_bytes=30 << 20
        ),
    )(pp, pw, dko, dvo, dkb, dvb, ds)


def body(queries, key_rows, value_rows, out_weight, sum_lists, out_grad):
    q, k, v, g = queries[0], key_rows[0], value_rows[0], out_grad[0]
    tails = jnp.stack([k[TOK - SUMC :], v[TOK - SUMC :]])
    strides = jnp.arange(FSDP, dtype=jnp.int32)
    block = lax.axis_index("fsdp") * 2 + jnp.arange(2, dtype=jnp.int32)
    named = jnp.any(sum_lists[0][:, :, None] == strides[None, None, :], axis=1)
    usable = named & ((strides[None, :] + 1) * STRIDE <= (block[:, None] - 2) * BLK)
    bias = jnp.where(usable, 0.0, NEG).astype(F32)
    bias = jnp.broadcast_to(bias.T[:, None, :, None], (FSDP, SUMC, 2, BLK)).reshape(TOK, TOK)
    wf, ga, pk, pv, sa = gather_inputs(out_weight, g, k, v, tails)
    pp, pw, dq, dko, dvo, dkb, dvb, ds = attend(q, k, v, pk, pv, sa, wf, ga, bias)
    proj, kg, vg, wg = reduce_gradients(pp, pw, dko, dvo, dkb, dvb, ds)
    return proj[None], dq[None], kg[None], vg[None], wg


def solution(mesh):
    tokens = P("dp", "fsdp", "head")
    return jax.shard_map(
        body,
        mesh=mesh,
        in_specs=(tokens, tokens, tokens, P("fsdp", "head"), P("dp", "fsdp", None), tokens),
        out_specs=(tokens, tokens, tokens, tokens, P("fsdp", "head")),
        check_vma=False,
    )
```

time: 560 us -> 129 us (0.23)
  the two profiles are of different devices: /device:TPU:6 before, /device:TPU:212 now
where the time goes in v1:
time: 129 us; the launch traced here: 128 us
  Pallas kernels  116 us (90%)
  local copies, waits for them, and re-layouts  10.9 us (8%)
    pallas_call x1, Pallas kernels, reduce_gradients(): pl.pallas_call(reduce_kernel, name='reduce_gradients', out_shape=(jax.Sha...  60.3 us
    pallas_call x1, Pallas kernels, gather_inputs(): pl.pallas_call(gather_kernel, name='gather_inputs', out_shape=(jax.ShapeD...  48.7 us
    unnamed x18, local copies, waits for them, and re-layouts  9.3 us
    pallas_call x1, Pallas kernels, attend(): pl.pallas_call(attend_kernel, name='attend', out_shape=(jax.ShapeDtypeStr...  7.02 us

profile of v1, /device:TPU:212, one launch (start us, length us, event | category | flops | bytes accessed | tf_op | source)
XLA Modules:
  0.0 128.5 jit_solution(6489965468912200719)
XLA Ops:
  0.6 0.8 fusion
  1.4 0.1 fusion.1
  1.5 0.7 slice.8
  2.2 0.7 slice.9
  2.9 0.1 copy.11
  3.0 0.1 broadcast_bitcast_fusion.bias_ref
  3.1 0.0 copy-start
  3.1 0.9 copy-done
  4.1 0.0 copy-start.2
  4.1 0.9 copy-done.2
  5.0 0.0 copy-start.5
  5.0 0.9 copy-done.5
  6.0 0.0 copy-start.6
  6.0 0.8 copy-done.6
  6.8 48.7 %gather_inputs.1 = (bf16[4,8,64,512]{3,2,1,0:T(8,128)(2,1)S(1)}, bf16[4,256,512]{2,1,0:T(8,128)(2,1)S(1)}, bf16[256,512]{1,0:T(8,128)(2,1)S(1)}, bf16[256,512]{1...) custom-call(bf16[64,512]{1,0:T(8,128)(2,1)S(1)} %copy-done.6, bf16[256,512]{1,0:T(8,128)(2,1)S(1)} %bitcast.20, ...), custom_call_target="tpu_custom_call" | custom-call | tf_op jit(solution)/shard_map/gather_inputs/pallas_call | solution.py:249
  55.5 0.0 copy-start.1
  55.5 0.9 copy-done.1
  56.5 0.0 copy-start.3
  56.5 0.9 copy-done.3
  57.4 0.0 copy-start.4
  57.4 0.9 copy-done.4
  58.4 7.0 %attend.1 = (bf16[4,256,512]{2,1,0:T(8,128)(2,1)S(1)}, bf16[4,8,64,512]{3,2,1,0:T(8,128)(2,1)S(1)}, bf16[256,512]{1,0:T(8,128)(2,1)}, f32[256,512]{1,0:T(8,128)S...) custom-call(bf16[256,512]{1,0:T(8,128)(2,1)S(1)} %bitcast.19, ...), custom_call_target="tpu_custom_call" | custom-call | tf_op jit(solution)/shard_map/attend/pallas_call | solution.py:347
  65.4 60.3 %reduce_gradients.1 = (bf16[256,512]{1,0:T(8,128)(2,1)S(1)}, bf16[256,512]{1,0:T(8,128)(2,1)S(1)}, bf16[256,512]{1,0:T(8,128)(2,1)S(1)}, f32[64,512]{1,0:T(8,128)S(1)}) custom-call(bf16[4,256,512]{2,1,0:T(8,128)(2,1)S(1)} %get-tuple-element.27.pp, bf16[4,8,64,512]{3,2,1,0:T(8,128)(2,1)S(1)} %get-tuple-element.28.pw, f32[256,512]{1,0:T(8,128)S(1)} %get-tuple-element.29.dko, ...), custom_call_target="tpu_custom_call" | custom-call | tf_op jit(solution)/shard_map/reduce_gradients/pallas_call | solution.py:545
  125.7 0.7 copy.16
  126.4 0.7 copy.17
  127.1 0.7 copy.18
  127.8 0.7 copy.19
  (3 shorter events, 0.0 us)
Async XLA Ops:
  3.1 1.0 copy-start
  4.1 0.9 copy-start.2
  5.0 0.9 copy-start.5
  6.0 0.8 copy-start.6
  55.5 1.0 copy-start.1
  56.5 0.9 copy-start.3
  57.4 0.9 copy-start.4

commit v2 on v1

v2 whole, which is shorter than its diff:
```python
import math

import jax
import jax.numpy as jnp
from jax import lax
from jax.experimental import pallas as pl
from jax.experimental.pallas import tpu as pltpu
from jax.sharding import PartitionSpec as P

HS = 128
BLK = 128
STRIDE = 256
SUMC = 8
NX = 4
NZ = 8
NH = 4
ND = 4
TOK = 256
WID = 512
ROWS = 64
HALF = ROWS // 2
HEADS = WID // HS
FSDP = NX * NZ
SCALE = 1.0 / math.sqrt(HS)
NEG = -1e30
MESH = pl.DeviceIdType.MESH
BF = jnp.bfloat16
F32 = jnp.float32


def place():
    d = lax.axis_index("dp")
    f = lax.axis_index("fsdp")
    h = lax.axis_index("head")
    return d, lax.div(f, NZ), lax.rem(f, NZ), h


def send(src, dst, ssem, rsem, dev):
    return pltpu.make_async_remote_copy(
        src_ref=src, dst_ref=dst, send_sem=ssem, recv_sem=rsem, device_id=dev, device_id_type=MESH
    )


def meet(bar, count, swapped):
    @pl.when(swapped)
    def _():
        pl.semaphore_wait(bar, count + 1)

    @pl.when(jnp.logical_not(swapped))
    def _():
        pl.semaphore_wait(bar, count)


class Links:
    def __init__(self):
        self.d, self.x, self.z, self.h = place()
        d, x, z, h = self.d, self.x, self.z, self.h
        self.xr, self.xl = lax.rem(x + 1, NX), lax.rem(x + NX - 1, NX)
        self.xo = lax.rem(x + 2, NX)
        self.zr, self.zl = lax.rem(z + 1, NZ), lax.rem(z + NZ - 1, NZ)
        f = x * NZ + z
        self.f = f
        self.sib = h + 1 - 2 * lax.rem(h, 2)
        self.rem = lax.rem(h + 2, NH)
        self.far = lax.rem(self.sib + 2, NH)
        self.dev_xr = (d, self.xr * NZ + z, h)
        self.dev_xl = (d, self.xl * NZ + z, h)
        self.dev_zr = (d, x * NZ + self.zr, h)
        self.dev_zl = (d, x * NZ + self.zl, h)
        self.dev_next = (d, lax.rem(f + 1, FSDP), h)
        self.dev_prev = (d, lax.rem(f + FSDP - 1, FSDP), h)
        self.dev_sib = (d, f, self.sib)
        self.dev_rem = (d, f, self.rem)
        self.dev_swap = (d, h * NZ + z, x)
        self.zs = [lax.rem(z + i, NZ) for i in range(NZ)]
        self.xs = [lax.rem(x + i, NX) for i in range(NX)]

    def dev_z(self, i):
        return (self.d, self.x * NZ + self.zs[i], self.h)

    def dev_x(self, i):
        return (self.d, self.xs[i] * NZ + self.z, self.h)


def vmem(n):
    return [pl.BlockSpec(memory_space=pltpu.VMEM)] * n


def dot_nt(a, b):
    return lax.dot_general(a, b, (((1,), (1,)), ((), ())), preferred_element_type=F32)


def dot_tn(a, b):
    return lax.dot_general(a, b, (((0,), (0,)), ((), ())), preferred_element_type=F32)


def dot_nn(a, b):
    return lax.dot_general(a, b, (((1,), (0,)), ((), ())), preferred_element_type=F32)


def step_kernel(
    w_ref, g_ref, q_ref, k_ref, v_ref, bias_ref,
    pown, pin, dq, dko, dvo, back, far, fin,
    wf, ga, qs, ks, vs, pk, pv, sa, sk, sv, wts, mxt, mx, pw, pp, gacc, gm, pfar, pmid, nb, ds,
    arm, bx, xrm, zin, zout, fout, sx, szo, szi,
    swap_sem, loc_sem, zr_s, zr_r, zl_s, zl_r, xr_s, xr_r, xl_s, xl_r, fr_s, fr_r, fl_s, fl_r,
    kv_s, kv_r, g_s, g_r, tz_s, tz_r, tx_s, tx_r,
    a_s, a_r, b_s, b_r, z_s, z_r, f_s, f_r, fl_sem, bk_s, bk_r, p_s, p_r, sx_s, sx_r, sz_s, sz_r,
):
    m = Links()
    d, x, z, h = m.d, m.x, m.z, m.h
    bar = pltpu.get_barrier_semaphore()

    def hello(dev):
        pl.semaphore_signal(bar, inc=1, device_id=dev, device_id_type=MESH)

    def owner(i):
        return (lax.rem(d + i, ND), h * NZ + z, x)

    swapped = x != h

    @pl.when(swapped)
    def _():
        hello(owner(0))

    hello(m.dev_rem)
    for i in range(1, ND):
        hello(owner(i))
    for i in range(1, NZ):
        hello(m.dev_z(i))
    for i in range(1, NX):
        hello(m.dev_x(i))
    hello(m.dev_sib)
    hello(m.dev_next)
    hello(m.dev_prev)
    local = [
        pltpu.make_async_copy(q_ref, qs, loc_sem.at[1]),
        pltpu.make_async_copy(k_ref, ks, loc_sem.at[2]),
        pltpu.make_async_copy(v_ref, vs, loc_sem.at[3]),
        pltpu.make_async_copy(g_ref, ga.at[h], loc_sem.at[4]),
        pltpu.make_async_copy(k_ref.at[pl.ds(TOK - SUMC, SUMC)], sa.at[x, z, 0], loc_sem.at[5]),
        pltpu.make_async_copy(v_ref.at[pl.ds(TOK - SUMC, SUMC)], sa.at[x, z, 1], loc_sem.at[6]),
    ]
    for c in local:
        c.start()
    meet(bar, (NZ - 1) + (NX - 1) + 4 + (ND - 1), swapped)

    def swap():
        return send(w_ref, wf.at[h, z], swap_sem.at[0], swap_sem.at[1], m.dev_swap)

    def stay():
        return pltpu.make_async_copy(w_ref, wf.at[x, z], loc_sem.at[0])

    @pl.when(swapped)
    def _():
        swap().start()

    @pl.when(jnp.logical_not(swapped))
    def _():
        stay().start()

    tz = []
    for i in range(1, NZ):
        for j, ref in enumerate((k_ref, v_ref)):
            c = send(
                ref.at[pl.ds(TOK - SUMC, SUMC)], sa.at[x, z, j], tz_s.at[j, i - 1], tz_r.at[j, i - 1], m.dev_z(i)
            )
            c.start()
            tz.append(c)
    kv = []
    for j, (ref, dst) in enumerate(((k_ref, pk), (v_ref, pv))):
        for i in range(TOK // ROWS):
            piece = pl.ds(i * ROWS, ROWS)
            kv.append(send(ref.at[piece], dst.at[piece], kv_s.at[j, i], kv_r.at[j, i], m.dev_next))
    kv[0].start()
    kv[1].start()
    g_sib = send(g_ref, ga.at[h], g_s.at[1], g_r.at[1], m.dev_sib)
    g_sib.start()
    g_rem = send(g_ref, ga.at[h], g_s.at[0], g_r.at[0], m.dev_rem)
    g_pass = send(ga.at[m.rem], ga.at[m.rem], g_s.at[2], g_r.at[2], m.dev_sib)

    @pl.when(swapped)
    def _():
        swap().wait_send()

    g_rem.start()

    @pl.when(swapped)
    def _():
        swap().wait_recv()

    @pl.when(jnp.logical_not(swapped))
    def _():
        stay().wait()

    order = [("own", 0), ("l", 1), ("r", 1), ("l", 2), ("r", 2), ("l", 3), ("r", 3), ("l", 4)]
    where = [z if kind == "own" else m.zs[NZ - s] if kind == "r" else m.zs[s] for kind, s in order]
    zrs, zls, xsd, xfd = {}, {}, {}, {}

    def zright(s):
        slot = wf.at[x, m.zs[(NZ - s) % NZ]]
        zrs[s] = send(slot, slot, zr_s.at[s], zr_r.at[s], m.dev_zr)
        zrs[s].start()

    def zleft(s):
        slot = wf.at[x, m.zs[s]]
        zls[s] = send(slot, slot, zl_s.at[s], zl_r.at[s], m.dev_zl)
        zls[s].start()

    def xsend(n):
        slot = wf.at[x, where[n]]
        xsd[n] = (
            send(slot, slot, xr_s.at[n], xr_r.at[n], m.dev_xr),
            send(slot, slot, xl_s.at[n], xl_r.at[n], m.dev_xl),
        )
        xsd[n][0].start()
        xsd[n][1].start()

    def arrive(n):
        kind, s = order[n]
        if kind == "own":
            zleft(0)
            zright(0)
            kv[2].start()
        elif kind == "r":
            zrs[s - 1].wait_recv()
            if s < 3:
                zright(s)
                kv[2 + s].start()
        else:
            zls[s - 1].wait_recv()
            if s < 4:
                zleft(s)
        xsend(n)

    def forward(n):
        a = wf.at[m.xl, where[n], pl.ds(0, HALF)]
        b = wf.at[m.xr, where[n], pl.ds(HALF, HALF)]
        xfd[n] = (
            send(a, a, fr_s.at[n], fr_r.at[n], m.dev_xr),
            send(b, b, fl_s.at[n], fl_r.at[n], m.dev_xl),
        )
        xsd[n][0].wait_recv()
        xfd[n][0].start()
        xsd[n][1].wait_recv()
        xfd[n][1].start()

    arrive(0)

    def fore(n):
        first = m.f == 0
        key_at = lax.broadcasted_iota(jnp.int32, (TOK, TOK), 0)
        query_at = lax.broadcasted_iota(jnp.int32, (TOK, TOK), 1)
        own_bias = jnp.where(key_at <= query_at, 0.0, NEG)
        low = jnp.where(query_at < BLK, 0, BLK) + jnp.where(first, 2 * TOK, 0)
        prior_bias = jnp.where(key_at >= low, 0.0, NEG)
        cols = pl.ds(n * HS, HS)
        q = qs[:, cols]
        keys = (pk[:, cols], ks[:, cols], sk[:, cols])
        values = (pv[:, cols], vs[:, cols], sv[:, cols])
        scores = [
            dot_nt(key, q) * SCALE + bias
            for key, bias in zip(keys, (prior_bias, own_bias, bias_ref[...]))
        ]
        peak = jnp.max(jnp.maximum(jnp.maximum(scores[0], scores[1]), scores[2]), axis=0, keepdims=True)
        raised = [jnp.exp(s - peak) for s in scores]
        scale = 1.0 / jnp.sum(raised[0] + raised[1] + raised[2], axis=0, keepdims=True)
        mixed_t = None
        for j in range(3):
            weight = raised[j] * scale
            wts[n, j] = weight
            term = dot_tn(values[j], weight.astype(BF))
            mixed_t = term if mixed_t is None else mixed_t + term
        mxt[cols, :] = mixed_t.astype(BF)
        mx[:, cols] = mixed_t.T.astype(BF)

    def hind(n):
        cols = pl.ds(n * HS, HS)
        q = qs[:, cols]
        keys = (pk[:, cols], ks[:, cols], sk[:, cols])
        values = (pv[:, cols], vs[:, cols], sv[:, cols])
        grad = gm[:, cols]
        delta = jnp.sum(grad.astype(F32).T * mxt[cols, :].astype(F32), axis=0, keepdims=True)
        dscore = [(wts[n, j] * (dot_nt(values[j], grad) - delta)).astype(BF) for j in range(3)]
        nb[0, n] = (dot_nn(dscore[0], q) * SCALE).astype(BF)
        nb[1, n] = dot_nn(wts[n, 0].astype(BF), grad).astype(BF)
        far_k = dot_nn(dscore[2], q) * SCALE
        ds[:, :, 0, :, cols] = far_k.reshape(NX, NZ, SUMC, HS).astype(BF)
        far_v = dot_nn(wts[n, 2].astype(BF), grad)
        ds[:, :, 1, :, cols] = far_v.reshape(NX, NZ, SUMC, HS).astype(BF)
        dko[:, cols] = dot_nn(dscore[1], q) * SCALE
        dvo[:, cols] = dot_nn(wts[n, 1].astype(BF), grad)
        dq_t = dot_tn(keys[0], dscore[0]) + dot_tn(keys[1], dscore[1]) + dot_tn(keys[2], dscore[2])
        dq[:, cols] = (dq_t.T * SCALE).astype(BF)

    arrive(1)
    arrive(2)
    forward(0)
    for c in local[4:]:
        c.wait()
    for c in tz:
        c.wait_recv()
    tx = []
    for i in range(1, NX):
        c = send(sa.at[x], sa.at[x], tx_s.at[i - 1], tx_r.at[i - 1], m.dev_x(i))
        c.start()
        tx.append(c)
    arrive(3)
    forward(1)
    arrive(4)
    for c in kv[5:]:
        c.start()
    forward(2)
    arrive(5)
    forward(3)
    arrive(6)
    forward(4)
    arrive(7)
    forward(5)
    for c in local[:3]:
        c.wait()
    g_rem.wait_recv()
    g_pass.start()
    for c in kv:
        c.wait_recv()
    for c in tx:
        c.wait_recv()
    sk[...] = sa[:, :, 0].astype(F32).reshape(TOK, WID).astype(BF)
    sv[...] = sa[:, :, 1].astype(F32).reshape(TOK, WID).astype(BF)
    fore(0)
    forward(6)
    fore(1)
    forward(7)
    fore(2)
    fore(3)

    def share(c):
        part = dot_nn(mxt[...], ga[c])
        pw[c] = part.astype(BF).reshape(NZ, ROWS, WID)

    rows = [m.zs[(i + 1) % NZ] for i in range(NZ)]

    def leg_a(n):
        r = rows[n]
        return (
            send(pw.at[m.xo, r, pl.ds(0, HALF)], arm.at[0, n], a_s.at[0, n], a_r.at[0, n], m.dev_xr),
            send(pw.at[m.xo, r, pl.ds(HALF, HALF)], arm.at[1, n], a_s.at[1, n], a_r.at[1, n], m.dev_xl),
        )

    def leg_b(n):
        return (
            send(bx.at[0, n], xrm.at[0, n], b_s.at[0, n], b_r.at[0, n], m.dev_xr),
            send(bx.at[1, n], xrm.at[1, n], b_s.at[1, n], b_r.at[1, n], m.dev_xl),
        )

    local[3].wait()
    g_sib.wait_recv()
    g_pass.wait_recv()
    share(m.xo)
    a_legs = [leg_a(n) for n in range(NZ)]
    for n in range(NZ):
        a_legs[n][0].start()
        a_legs[n][1].start()
    share(m.xr)
    share(m.xl)
    share(x)
    b_legs, z_legs = {}, {}

    def stage_b(n):
        r = rows[n]
        a_legs[n][0].wait_recv()
        bx[0, n, pl.ds(0, HALF)] = (
            arm[0, n].astype(F32) + pw[m.xr, r, pl.ds(0, HALF)].astype(F32)
        ).astype(BF)
        bx[0, n, pl.ds(HALF, HALF)] = pw[m.xr, r, pl.ds(HALF, HALF)]
        a_legs[n][1].wait_recv()
        bx[1, n, pl.ds(0, HALF)] = pw[m.xl, r, pl.ds(0, HALF)]
        bx[1, n, pl.ds(HALF, HALF)] = (
            arm[1, n].astype(F32) + pw[m.xl, r, pl.ds(HALF, HALF)].astype(F32)
        ).astype(BF)
        b_legs[n] = leg_b(n)
        b_legs[n][0].start()
        b_legs[n][1].start()

    def stage_z(n):
        b_legs[n][0].wait_recv()
        b_legs[n][1].wait_recv()
        zout[n] = (
            xrm[0, n].astype(F32) + xrm[1, n].astype(F32) + pw[x, rows[n]].astype(F32)
        ).astype(BF)
        if n < NZ - 1:
            z_legs[n] = send(zout.at[n], zin.at[n], z_s.at[n], z_r.at[n], m.dev_z(n + 1))
            z_legs[n].start()

    def wide(c):
        return wf[c].reshape(WID, WID)

    gacc[...] = dot_nt(ga[x], wide(x)) + dot_nt(ga[m.xr], wide(m.xr)) + dot_nt(ga[m.xl], wide(m.xl))
    for c in (x, m.xr, m.xl):
        pp[c] = dot_nn(mx[...], wide(c)).astype(BF)
    for n in range(NZ):
        xfd[n][0].wait_recv()
        xfd[n][1].wait_recv()
    gm[...] = (gacc[...] + dot_nt(ga[m.xo], wide(m.xo))).astype(BF)
    pp[m.xo] = dot_nn(mx[...], wide(m.xo)).astype(BF)
    p_legs = [
        send(pp.at[m.far], pfar, p_s.at[0], p_r.at[0], m.dev_sib),
        send(pp.at[m.sib], pin.at[0], p_s.at[1], p_r.at[1], m.dev_sib),
        send(pmid, pin.at[1], p_s.at[2], p_r.at[2], m.dev_rem),
    ]
    p_legs[0].start()
    p_legs[1].start()
    bk = []

    def neighbour(n):
        for j in range(2):
            c = send(nb.at[j, n], back.at[j, n], bk_s.at[j, n], bk_r.at[j, n], m.dev_prev)
            c.start()
            bk.append(c)

    hind(0)
    hind(1)
    neighbour(0)
    p_legs[0].wait_recv()
    pmid[...] = (pfar[...].astype(F32) + pp[m.rem].astype(F32)).astype(BF)
    hind(2)
    neighbour(1)
    p_legs[2].start()
    hind(3)
    neighbour(2)
    for n in range(NZ):
        stage_b(n)
    neighbour(3)
    s_legs = [
        send(ds.at[m.xs[i]], sx.at[i - 1], sx_s.at[i - 1], sx_r.at[i - 1], m.dev_x(i)) for i in range(1, NX)
    ]
    for c in s_legs:
        c.start()
    stage_z(0)
    stage_z(1)
    stage_z(2)
    stage_z(3)
    stage_z(4)
    stage_z(5)
    stage_z(6)
    stage_z(7)
    pown[...] = pp[h]
    for c in s_legs:
        c.wait_recv()
    szo[...] = (
        (ds[x].astype(F32) + sx[0].astype(F32)) + (sx[1].astype(F32) + sx[2].astype(F32))
    ).astype(BF)
    t_legs = [
        send(szo.at[m.zs[i]], szi.at[i - 1], sz_s.at[i - 1], sz_r.at[i - 1], m.dev_z(i)) for i in range(1, NZ)
    ]
    for c in t_legs:
        c.start()
    total = zout[NZ - 1].astype(F32)
    for n in range(NZ - 1):
        z_legs[n].wait_recv()
        total += zin[n].astype(F32)
    fout[...] = total.astype(BF)
    f_legs = [send(fout, fin.at[i], f_s.at[i], f_r.at[i], owner(i)) for i in range(ND)]

    def keep_own():
        return pltpu.make_async_copy(fout, fin.at[0], fl_sem)

    for i in range(1, ND):
        f_legs[i].start()

    @pl.when(swapped)
    def _():
        f_legs[0].start()

    @pl.when(jnp.logical_not(swapped))
    def _():
        keep_own().start()

    own = szo[z].astype(F32)
    for i in range(NZ - 1):
        t_legs[i].wait_recv()
        own += szi[i].astype(F32)
    far[...] = own
    for c in bk:
        c.wait()
    p_legs[1].wait_recv()
    p_legs[2].wait_recv()
    for c in tz + kv + [g_sib, g_rem, g_pass] + tx + s_legs + p_legs + t_legs:
        c.wait_send()
    for c in list(zrs.values()) + list(zls.values()) + list(z_legs.values()):
        c.wait_send()
    for n in range(NZ):
        for c in (*xsd[n], *xfd[n], *a_legs[n], *b_legs[n]):
            c.wait_send()
    for i in range(1, ND):
        f_legs[i].wait()

    @pl.when(swapped)
    def _():
        f_legs[0].wait()

    @pl.when(jnp.logical_not(swapped))
    def _():
        keep_own().wait()


def step(w, g, q, k, v, bias):
    dma = pltpu.SemaphoreType.DMA
    shape = jax.ShapeDtypeStruct
    hbm = [pl.BlockSpec(memory_space=pltpu.HBM)] * 5
    buf = pltpu.VMEM
    return pl.pallas_call(
        step_kernel,
        name="step",
        out_shape=(
            shape((TOK, WID), BF),
            shape((2, TOK, WID), BF),
            shape((TOK, WID), BF),
            shape((TOK, WID), F32),
            shape((TOK, WID), F32),
            shape((2, HEADS, TOK, HS), BF),
            shape((2, SUMC, WID), F32),
            shape((ND, ROWS, WID), BF),
        ),
        in_specs=hbm + vmem(1),
        out_specs=tuple(vmem(8)),
        scratch_shapes=[
            buf((NX, NZ, ROWS, WID), BF),
            buf((NH, TOK, WID), BF),
            buf((TOK, WID), BF),
            buf((TOK, WID), BF),
            buf((TOK, WID), BF),
            buf((TOK, WID), BF),
            buf((TOK, WID), BF),
            buf((NX, NZ, 2, SUMC, WID), BF),
            buf((TOK, WID), BF),
            buf((TOK, WID), BF),
            buf((HEADS, 3, TOK, TOK), F32),
            buf((WID, TOK), BF),
            buf((TOK, WID), BF),
            buf((NH, NZ, ROWS, WID), BF),
            buf((NH, TOK, WID), BF),
            buf((TOK, WID), F32),
            buf((TOK, WID), BF),
            buf((TOK, WID), BF),
            buf((TOK, WID), BF),
            buf((2, HEADS, TOK, HS), BF),
            buf((NX, NZ, 2, SUMC, WID), BF),
            buf((2, NZ, HALF, WID), BF),
            buf((2, NZ, ROWS, WID), BF),
            buf((2, NZ, ROWS, WID), BF),
            buf((NZ - 1, ROWS, WID), BF),
            buf((NZ, ROWS, WID), BF),
            buf((ROWS, WID), BF),
            buf((NX - 1, NZ, 2, SUMC, WID), BF),
            buf((NZ, 2, SUMC, WID), BF),
            buf((NZ - 1, 2, SUMC, WID), BF),
        ]
        + [dma((2,)), dma((7,))]
        + [dma((3,)), dma((3,)), dma((4,)), dma((4,))]
        + [dma((NZ,))] * 8
        + [dma((2, TOK // ROWS))] * 2
        + [dma((3,)), dma((3,))]
        + [dma((2, NZ - 1)), dma((2, NZ - 1)), dma((NX - 1,)), dma((NX - 1,))]
        + [dma((2, NZ))] * 4
        + [dma((NZ - 1,)), dma((NZ - 1,)), dma((ND,)), dma((ND,)), dma]
        + [dma((2, HEADS)), dma((2, HEADS)), dma((3,)), dma((3,))]
        + [dma((NX - 1,)), dma((NX - 1,)), dma((NZ - 1,)), dma((NZ - 1,))],
        compiler_params=pltpu.CompilerParams(
            collective_id=0, has_side_effects=True, vmem_limit_bytes=36 << 20
        ),
    )(*(pltpu.with_memory_space_constraint(a, pltpu.HBM) for a in (w, g, q, k, v)), bias)


def finish_kernel(pown, pin, dq, dko, dvo, back, far, fin, proj, qg, kg, vg, wg):
    proj[...] = (pown[...].astype(F32) + pin[0].astype(F32) + pin[1].astype(F32)).astype(BF)
    qg[...] = dq[...]
    for j, (out, mine) in enumerate(((kg, dko), (vg, dvo))):
        for n in range(HEADS):
            cols = pl.ds(n * HS, HS)
            out[pl.ds(0, TOK - 16), cols] = (
                mine[pl.ds(0, TOK - 16), cols] + back[j, n, pl.ds(0, TOK - 16)].astype(F32)
            ).astype(BF)
            tail = mine[pl.ds(TOK - 16, 16), cols] + back[j, n, pl.ds(TOK - 16, 16)].astype(F32)
            tail += jnp.concatenate([jnp.zeros((SUMC, HS), F32), far[j, :, cols]], axis=0)
            out[pl.ds(TOK - 16, 16), cols] = tail.astype(BF)
    wg[...] = (fin[0].astype(F32) + fin[1].astype(F32)) + (fin[2].astype(F32) + fin[3].astype(F32))


def finish(*parts):
    return pl.pallas_call(
        finish_kernel,
        name="finish",
        out_shape=(jax.ShapeDtypeStruct((TOK, WID), BF),) * 4 + (jax.ShapeDtypeStruct((ROWS, WID), F32),),
        in_specs=vmem(8),
        compiler_params=pltpu.CompilerParams(vmem_limit_bytes=16 << 20),
    )(*parts)


def body(queries, key_rows, value_rows, out_weight, sum_lists, out_grad):
    q, k, v, g = queries[0], key_rows[0], value_rows[0], out_grad[0]
    strides = jnp.arange(FSDP, dtype=jnp.int32)
    block = lax.axis_index("fsdp") * 2 + jnp.arange(2, dtype=jnp.int32)
    named = jnp.any(sum_lists[0][:, :, None] == strides[None, None, :], axis=1)
    usable = named & ((strides[None, :] + 1) * STRIDE <= (block[:, None] - 2) * BLK)
    bias = jnp.where(usable, 0.0, NEG).astype(F32)
    bias = jnp.broadcast_to(bias.T[:, None, :, None], (FSDP, SUMC, 2, BLK)).reshape(TOK, TOK)
    proj, qg, kg, vg, wg = finish(*step(out_weight, g, q, k, v, bias))
    return proj[None], qg[None], kg[None], vg[None], wg


def solution(mesh):
    tokens = P("dp", "fsdp", "head")
    return jax.shard_map(
        body,
        mesh=mesh,
        in_specs=(tokens, tokens, tokens, P("fsdp", "head"), P("dp", "fsdp", None), tokens),
        out_specs=(tokens, tokens, tokens, tokens, P("fsdp", "head")),
        check_vma=False,
    )
```

time: 129 us -> 99.6 us (0.77)
  the two profiles are of different devices: /device:TPU:212 before, /device:TPU:20 now
where the time goes in v2:
time: 99.6 us; the launch traced here: 99.4 us
  Pallas kernels  97.7 us (98%)
    pallas_call x1, Pallas kernels, step(): pl.pallas_call(step_kernel, name='step', out_shape=(shape((TOK, WID), BF)...  96.5 us

profile of v2, /device:TPU:20, one launch (start us, length us, event | category | flops | bytes accessed | tf_op | source)
XLA Modules:
  0.0 99.4 jit_solution(17638889247269922816)
XLA Ops:
  0.6 0.0 copy-start
  0.7 0.7 copy-done
  1.3 0.1 fusion
  1.4 0.1 fusion.1
  1.5 0.1 copy.11
  1.6 0.1 broadcast_bitcast_fusion.bias_ref
  1.7 96.5 %step.1 = (bf16[256,512]{1,0:T(8,128)(2,1)S(1)}, bf16[2,256,512]{2,1,0:T(8,128)(2,1)S(1)}, bf16[256,512]{1,0:T(8,128)(2,1)S(1)}, f32[256,512]{1,0:T(8,128)S(1)},...) custom-call(bf16[64,512]{1,0:T(8,128)(2,1)} %w_ref.1, ...), custom_call_target="tpu_custom_call" | custom-call | tf_op jit(solution)/shard_map/step/pallas_call | solution.py:512
  98.2 1.2 %finish.1 = (bf16[256,512]{1,0:T(8,128)(2,1)}, bf16[256,512]{1,0:T(8,128)(2,1)}, bf16[256,512]{1,0:T(8,128)(2,1)}, bf16[256,512]{1,0:T(8,128)(2,1)}, f32[64,512]{1,0:T(8,128)}) custom-call(bf16[256,512]{1,0:T(8,128)(2,1)S(1)} %get-tuple-element.18.pown, bf16[2,256,512]{2,1,0:T(8,128)(2,1)S(1)} %get-tuple-element.19.pin, ...), custom_call_target="tpu_custom_call" | custom-call | tf_op jit(solution)/shard_map/finish/pallas_call | solution.py:591
  (2 shorter events, 0.0 us)
Async XLA Ops:
  0.6 0.7 copy-start

commit v3 on v2

--- a/solution.py
+++ b/solution.py
@@ -174,6 +174,7 @@
             kv.append(send(ref.at[piece], dst.at[piece], kv_s.at[j, i], kv_r.at[j, i], m.dev_next))
     kv[0].start()
     kv[1].start()
+    kv[2].start()
     g_sib = send(g_ref, ga.at[h], g_s.at[1], g_r.at[1], m.dev_sib)
     g_sib.start()
     g_rem = send(g_ref, ga.at[h], g_s.at[0], g_r.at[0], m.dev_rem)
@@ -221,12 +222,12 @@
         if kind == "own":
             zleft(0)
             zright(0)
-            kv[2].start()
+            kv[3].start()
         elif kind == "r":
             zrs[s - 1].wait_recv()
             if s < 3:
                 zright(s)
-                kv[2 + s].start()
+                kv[3 + s].start()
         else:
             zls[s - 1].wait_recv()
             if s < 4:
@@ -293,9 +294,6 @@
         dq_t = dot_tn(keys[0], dscore[0]) + dot_tn(keys[1], dscore[1]) + dot_tn(keys[2], dscore[2])
         dq[:, cols] = (dq_t.T * SCALE).astype(BF)
 
-    arrive(1)
-    arrive(2)
-    forward(0)
     for c in local[4:]:
         c.wait()
     for c in tz:
@@ -305,18 +303,19 @@
         c = send(sa.at[x], sa.at[x], tx_s.at[i - 1], tx_r.at[i - 1], m.dev_x(i))
         c.start()
         tx.append(c)
+    arrive(1)
+    arrive(2)
+    forward(0)
     arrive(3)
+    arrive(4)
+    for c in kv[6:]:
+        c.start()
     forward(1)
-    arrive(4)
-    for c in kv[5:]:
-        c.start()
+    arrive(5)
     forward(2)
-    arrive(5)
+    arrive(6)
     forward(3)
-    arrive(6)
-    forward(4)
     arrive(7)
-    forward(5)
     for c in local[:3]:
         c.wait()
     g_rem.wait_recv()
@@ -327,18 +326,21 @@
         c.wait_recv()
     sk[...] = sa[:, :, 0].astype(F32).reshape(TOK, WID).astype(BF)
     sv[...] = sa[:, :, 1].astype(F32).reshape(TOK, WID).astype(BF)
+    forward(4)
     fore(0)
+    forward(5)
+    fore(1)
     forward(6)
-    fore(1)
+    fore(2)
     forward(7)
-    fore(2)
     fore(3)
 
     def share(c):
         part = dot_nn(mxt[...], ga[c])
         pw[c] = part.astype(BF).reshape(NZ, ROWS, WID)
 
-    rows = [m.zs[(i + 1) % NZ] for i in range(NZ)]
+    away = (4, 3, 5, 2, 6, 1, 7, 0)
+    rows = [m.zs[i] for i in away]
 
     def leg_a(n):
         r = rows[n]
@@ -385,12 +387,13 @@
     def stage_z(n):
         b_legs[n][0].wait_recv()
         b_legs[n][1].wait_recv()
-        zout[n] = (
-            xrm[0, n].astype(F32) + xrm[1, n].astype(F32) + pw[x, rows[n]].astype(F32)
-        ).astype(BF)
-        if n < NZ - 1:
-            z_legs[n] = send(zout.at[n], zin.at[n], z_s.at[n], z_r.at[n], m.dev_z(n + 1))
-            z_legs[n].start()
+        part = xrm[0, n].astype(F32) + xrm[1, n].astype(F32) + pw[x, rows[n]].astype(F32)
+        if n == NZ - 1:
+            return part
+        zout[n] = part.astype(BF)
+        z_legs[n] = send(zout.at[n], zin.at[n], z_s.at[n], z_r.at[n], m.dev_z(away[n]))
+        z_legs[n].start()
+        return None
 
     def wide(c):
         return wf[c].reshape(WID, WID)
@@ -412,38 +415,50 @@
     p_legs[1].start()
     bk = []
 
-    def neighbour(n):
-        for j in range(2):
-            c = send(nb.at[j, n], back.at[j, n], bk_s.at[j, n], bk_r.at[j, n], m.dev_prev)
-            c.start()
-            bk.append(c)
+    def neighbour(j, n):
+        c = send(nb.at[j, n], back.at[j, n], bk_s.at[j, n], bk_r.at[j, n], m.dev_prev)
+        c.start()
+        bk.append(c)
 
     hind(0)
     hind(1)
-    neighbour(0)
+    hind(2)
+    hind(3)
     p_legs[0].wait_recv()
     pmid[...] = (pfar[...].astype(F32) + pp[m.rem].astype(F32)).astype(BF)
-    hind(2)
-    neighbour(1)
-    p_legs[2].start()
-    hind(3)
-    neighbour(2)
     for n in range(NZ):
         stage_b(n)
-    neighbour(3)
+    p_legs[2].start()
     s_legs = [
         send(ds.at[m.xs[i]], sx.at[i - 1], sx_s.at[i - 1], sx_r.at[i - 1], m.dev_x(i)) for i in range(1, NX)
     ]
     for c in s_legs:
         c.start()
-    stage_z(0)
-    stage_z(1)
-    stage_z(2)
-    stage_z(3)
-    stage_z(4)
-    stage_z(5)
-    stage_z(6)
-    stage_z(7)
+    for n in range(NZ - 1):
+        stage_z(n)
+    total = stage_z(NZ - 1)
+    neighbour(0, 0)
+    neighbour(1, 0)
+    for n in range(NZ - 1):
+        z_legs[n].wait_recv()
+        total += zin[n].astype(F32)
+    fout[...] = total.astype(BF)
+    f_legs = [send(fout, fin.at[i], f_s.at[i], f_r.at[i], owner(i)) for i in range(ND)]
+
+    def keep_own():
+        return pltpu.make_async_copy(fout, fin.at[0], fl_sem)
+
+    for i in range(1, ND):
+        f_legs[i].start()
+
+    @pl.when(swapped)
+    def _():
+        f_legs[0].start()
+
+    @pl.when(jnp.logical_not(swapped))
+    def _():
+        keep_own().start()
+
     pown[...] = pp[h]
     for c in s_legs:
         c.wait_recv()
@@ -455,27 +470,9 @@
     ]
     for c in t_legs:
         c.start()
-    total = zout[NZ - 1].astype(F32)
-    for n in range(NZ - 1):
-        z_legs[n].wait_recv()
-        total += zin[n].astype(F32)
-    fout[...] = total.astype(BF)
-    f_legs = [send(fout, fin.at[i], f_s.at[i], f_r.at[i], owner(i)) for i in range(ND)]
-
-    def keep_own():
-        return pltpu.make_async_copy(fout, fin.at[0], fl_sem)
-
-    for i in range(1, ND):
-        f_legs[i].start()
-
-    @pl.when(swapped)
-    def _():
-        f_legs[0].start()
-
-    @pl.when(jnp.logical_not(swapped))
-    def _():
-        keep_own().start()
-
+    for n in range(1, HEADS):
+        neighbour(0, n)
+        neighbour(1, n)
     own = szo[z].astype(F32)
     for i in range(NZ - 1):
         t_legs[i].wait_recv()
@@ -550,7 +547,7 @@
             buf((2, NZ, ROWS, WID), BF),
             buf((2, NZ, ROWS, WID), BF),
             buf((NZ - 1, ROWS, WID), BF),
-            buf((NZ, ROWS, WID), BF),
+            buf((NZ - 1, ROWS, WID), BF),
             buf((ROWS, WID), BF),
             buf((NX - 1, NZ, 2, SUMC, WID), BF),
             buf((NZ, 2, SUMC, WID), BF),

time: 99.6 us -> 97.6 us (0.980)
  the two profiles are of different devices: /device:TPU:20 before, /device:TPU:6 now
where the time goes in v3:
time: 97.6 us; the launch traced here: 96.3 us
  Pallas kernels  94.6 us (97%)
    pallas_call x1, Pallas kernels, step(): pl.pallas_call(step_kernel, name='step', out_shape=(shape((TOK, WID), BF)...  93.4 us

profile of v3, /device:TPU:6, one launch (start us, length us, event | category | flops | bytes accessed | tf_op | source)
XLA Modules:
  0.0 96.3 jit_solution(18208455257131250621)
XLA Ops:
  0.6 0.0 copy-start
  0.7 0.7 copy-done
  1.3 0.1 fusion
  1.4 0.1 fusion.1
  1.5 0.1 copy.11
  1.6 0.1 broadcast_bitcast_fusion.bias_ref
  1.7 93.4 %step.1 = (bf16[256,512]{1,0:T(8,128)(2,1)S(1)}, bf16[2,256,512]{2,1,0:T(8,128)(2,1)S(1)}, bf16[256,512]{1,0:T(8,128)(2,1)S(1)}, f32[256,512]{1,0:T(8,128)S(1)},...) custom-call(bf16[64,512]{1,0:T(8,128)(2,1)} %w_ref.1, ...), custom_call_target="tpu_custom_call" | custom-call | tf_op jit(solution)/shard_map/step/pallas_call | solution.py:509
  95.2 1.2 %finish.1 = (bf16[256,512]{1,0:T(8,128)(2,1)}, bf16[256,512]{1,0:T(8,128)(2,1)}, bf16[256,512]{1,0:T(8,128)(2,1)}, bf16[256,512]{1,0:T(8,128)(2,1)}, f32[64,512]{1,0:T(8,128)}) custom-call(bf16[256,512]{1,0:T(8,128)(2,1)S(1)} %get-tuple-element.18.pown, bf16[2,256,512]{2,1,0:T(8,128)(2,1)S(1)} %get-tuple-element.19.pin, ...), custom_call_target="tpu_custom_call" | custom-call | tf_op jit(solution)/shard_map/finish/pallas_call | solution.py:588
  (2 shorter events, 0.0 us)
Async XLA Ops:
  0.6 0.7 copy-start

commit v4 on v3

--- a/solution.py
+++ b/solution.py
@@ -102,9 +102,9 @@
     w_ref, g_ref, q_ref, k_ref, v_ref, bias_ref,
     pown, pin, dq, dko, dvo, back, far, fin,
     wf, ga, qs, ks, vs, pk, pv, sa, sk, sv, wts, mxt, mx, pw, pp, gacc, gm, pfar, pmid, nb, ds,
-    arm, bx, xrm, zin, zout, fout, sx, szo, szi,
+    arm, bx, xrm, zin, zout, fout, sx, szo, szi, rv,
     swap_sem, loc_sem, zr_s, zr_r, zl_s, zl_r, xr_s, xr_r, xl_s, xl_r, fr_s, fr_r, fl_s, fl_r,
-    kv_s, kv_r, g_s, g_r, tz_s, tz_r, tx_s, tx_r,
+    kv_s, kv_r, g_s, g_r, tr_s, tr_r, tl_s, tl_r, tx_s, tx_r, rv_s, rv_r, rf_s,
     a_s, a_r, b_s, b_r, z_s, z_r, f_s, f_r, fl_sem, bk_s, bk_r, p_s, p_r, sx_s, sx_r, sz_s, sz_r,
 ):
     m = Links()
@@ -159,19 +159,40 @@
     def _():
         stay().start()
 
-    tz = []
-    for i in range(1, NZ):
+    tx = []
+    for i in range(1, NX):
         for j, ref in enumerate((k_ref, v_ref)):
             c = send(
-                ref.at[pl.ds(TOK - SUMC, SUMC)], sa.at[x, z, j], tz_s.at[j, i - 1], tz_r.at[j, i - 1], m.dev_z(i)
+                ref.at[pl.ds(TOK - SUMC, SUMC)], sa.at[x, z, j], tx_s.at[j, i - 1], tx_r.at[j, i - 1], m.dev_x(i)
             )
             c.start()
-            tz.append(c)
+            tx.append(c)
     kv = []
     for j, (ref, dst) in enumerate(((k_ref, pk), (v_ref, pv))):
         for i in range(TOK // ROWS):
             piece = pl.ds(i * ROWS, ROWS)
             kv.append(send(ref.at[piece], dst.at[piece], kv_s.at[j, i], kv_r.at[j, i], m.dev_next))
+    wraps = z == NZ - 1
+    pieces = [pl.ds(i * ROWS, ROWS) for i in range(TOK // ROWS)]
+    hop = [send(v_ref.at[p], rv.at[p], rv_s.at[i], rv_r.at[i], m.dev_xr) for i, p in enumerate(pieces)]
+    hand = [send(rv.at[p], pv.at[p], rf_s.at[i], kv_r.at[1, i], m.dev_zr) for i, p in enumerate(pieces)]
+
+    @pl.when(wraps)
+    def _():
+        for c in hop:
+            c.start()
+
+    def values(i):
+        @pl.when(jnp.logical_not(wraps))
+        def _():
+            kv[4 + i].start()
+
+    def hand_on(i):
+        @pl.when(wraps)
+        def _():
+            hop[i].wait_recv()
+            hand[i].start()
+
     kv[0].start()
     kv[1].start()
     kv[2].start()
@@ -198,15 +219,23 @@
     where = [z if kind == "own" else m.zs[NZ - s] if kind == "r" else m.zs[s] for kind, s in order]
     zrs, zls, xsd, xfd = {}, {}, {}, {}
 
+    tzr, tzl = {}, {}
+
     def zright(s):
-        slot = wf.at[x, m.zs[(NZ - s) % NZ]]
+        at = m.zs[(NZ - s) % NZ]
+        slot = wf.at[x, at]
         zrs[s] = send(slot, slot, zr_s.at[s], zr_r.at[s], m.dev_zr)
         zrs[s].start()
+        slab = sa.at[:, at]
+        tzr[s] = send(slab, slab, tr_s.at[s], tr_r.at[s], m.dev_zr)
 
     def zleft(s):
-        slot = wf.at[x, m.zs[s]]
+        at = m.zs[s]
+        slot = wf.at[x, at]
         zls[s] = send(slot, slot, zl_s.at[s], zl_r.at[s], m.dev_zl)
         zls[s].start()
+        slab = sa.at[:, at]
+        tzl[s] = send(slab, slab, tl_s.at[s], tl_r.at[s], m.dev_zl)
 
     def xsend(n):
         slot = wf.at[x, where[n]]
@@ -222,17 +251,35 @@
         if kind == "own":
             zleft(0)
             zright(0)
-            kv[3].start()
         elif kind == "r":
             zrs[s - 1].wait_recv()
             if s < 3:
                 zright(s)
-                kv[3 + s].start()
         else:
             zls[s - 1].wait_recv()
             if s < 4:
                 zleft(s)
         xsend(n)
+
+    def summaries(n):
+        kind, s = order[n]
+        if kind == "own":
+            for c in local[4:]:
+                c.wait()
+            for c in tx:
+                c.wait_recv()
+            tzl[0].start()
+            tzr[0].start()
+            kv[3].start()
+        elif kind == "r":
+            tzr[s - 1].wait_recv()
+            if s < 3:
+                tzr[s].start()
+                values(s - 1)
+        else:
+            tzl[s - 1].wait_recv()
+            if s < 4:
+                tzl[s].start()
 
     def forward(n):
         a = wf.at[m.xl, where[n], pl.ds(0, HALF)]
@@ -294,39 +341,40 @@
         dq_t = dot_tn(keys[0], dscore[0]) + dot_tn(keys[1], dscore[1]) + dot_tn(keys[2], dscore[2])
         dq[:, cols] = (dq_t.T * SCALE).astype(BF)
 
-    for c in local[4:]:
-        c.wait()
-    for c in tz:
-        c.wait_recv()
-    tx = []
-    for i in range(1, NX):
-        c = send(sa.at[x], sa.at[x], tx_s.at[i - 1], tx_r.at[i - 1], m.dev_x(i))
-        c.start()
-        tx.append(c)
+    summaries(0)
+    hand_on(0)
+    hand_on(1)
     arrive(1)
     arrive(2)
+    hand_on(2)
+    hand_on(3)
+    summaries(1)
+    summaries(2)
     forward(0)
     arrive(3)
     arrive(4)
-    for c in kv[6:]:
-        c.start()
     forward(1)
+    summaries(3)
+    summaries(4)
+    values(2)
+    values(3)
     arrive(5)
     forward(2)
     arrive(6)
     forward(3)
+    summaries(5)
+    summaries(6)
     arrive(7)
+    forward(4)
     for c in local[:3]:
         c.wait()
     g_rem.wait_recv()
     g_pass.start()
+    summaries(7)
     for c in kv:
-        c.wait_recv()
-    for c in tx:
         c.wait_recv()
     sk[...] = sa[:, :, 0].astype(F32).reshape(TOK, WID).astype(BF)
     sv[...] = sa[:, :, 1].astype(F32).reshape(TOK, WID).astype(BF)
-    forward(4)
     fore(0)
     forward(5)
     fore(1)
@@ -482,8 +530,21 @@
         c.wait()
     p_legs[1].wait_recv()
     p_legs[2].wait_recv()
-    for c in tz + kv + [g_sib, g_rem, g_pass] + tx + s_legs + p_legs + t_legs:
+    for c in tx + kv[:4] + [g_sib, g_rem, g_pass] + s_legs + p_legs + t_legs:
         c.wait_send()
+    for c in list(tzr.values()) + list(tzl.values()):
+        c.wait_send()
+
+    @pl.when(wraps)
+    def _():
+        for c in hop + hand:
+            c.wait_send()
+
+    @pl.when(jnp.logical_not(wraps))
+    def _():
+        for c in kv[4:]:
+            c.wait_send()
+
     for c in list(zrs.values()) + list(zls.values()) + list(z_legs.values()):
         c.wait_send()
     for n in range(NZ):
@@ -552,13 +613,15 @@
             buf((NX - 1, NZ, 2, SUMC, WID), BF),
             buf((NZ, 2, SUMC, WID), BF),
             buf((NZ - 1, 2, SUMC, WID), BF),
+            buf((TOK, WID), BF),
         ]
         + [dma((2,)), dma((7,))]
         + [dma((3,)), dma((3,)), dma((4,)), dma((4,))]
         + [dma((NZ,))] * 8
         + [dma((2, TOK // ROWS))] * 2
         + [dma((3,)), dma((3,))]
-        + [dma((2, NZ - 1)), dma((2, NZ - 1)), dma((NX - 1,)), dma((NX - 1,))]
+        + [dma((3,)), dma((3,)), dma((4,)), dma((4,)), dma((2, NX - 1)), dma((2, NX - 1))]
+        + [dma((TOK // ROWS,))] * 3
         + [dma((2, NZ))] * 4
         + [dma((NZ - 1,)), dma((NZ - 1,)), dma((ND,)), dma((ND,)), dma]
         + [dma((2, HEADS)), dma((2, HEADS)), dma((3,)), dma((3,))]

time: 97.6 us -> 95 us (0.973); the launches traced: 96.3 us -> 94.9 us
  Pallas kernels: 94.6 us -> 93.1 us
    pallas_call x1, Pallas kernels: 93.4 us -> 91.9 us  [step(): pl.pallas_call(step_kernel, name='step', out_shape=(shape((TOK, WID), BF)...]
where the time goes in v4:
time: 95 us; the launch traced here: 94.9 us
  Pallas kernels  93.1 us (98%)
    pallas_call x1, Pallas kernels, step(): pl.pallas_call(step_kernel, name='step', out_shape=(shape((TOK, WID), BF)...  91.9 us

profile of v4, /device:TPU:6, one launch (start us, length us, event | category | flops | bytes accessed | tf_op | source)
XLA Modules:
  0.0 94.9 jit_solution(13491214986582385007)
XLA Ops:
  0.6 0.0 copy-start
  0.7 0.7 copy-done
  1.3 0.1 fusion
  1.4 0.1 fusion.1
  1.5 0.1 copy.11
  1.6 0.1 broadcast_bitcast_fusion.bias_ref
  1.7 91.9 %step.1 = (bf16[256,512]{1,0:T(8,128)(2,1)S(1)}, bf16[2,256,512]{2,1,0:T(8,128)(2,1)S(1)}, bf16[256,512]{1,0:T(8,128)(2,1)S(1)}, f32[256,512]{1,0:T(8,128)S(1)},...) custom-call(bf16[64,512]{1,0:T(8,128)(2,1)} %w_ref.1, ...), custom_call_target="tpu_custom_call" | custom-call | tf_op jit(solution)/shard_map/step/pallas_call | solution.py:570
  93.7 1.2 %finish.1 = (bf16[256,512]{1,0:T(8,128)(2,1)}, bf16[256,512]{1,0:T(8,128)(2,1)}, bf16[256,512]{1,0:T(8,128)(2,1)}, bf16[256,512]{1,0:T(8,128)(2,1)}, f32[64,512]{1,0:T(8,128)}) custom-call(bf16[256,512]{1,0:T(8,128)(2,1)S(1)} %get-tuple-element.18.pown, bf16[2,256,512]{2,1,0:T(8,128)(2,1)S(1)} %get-tuple-element.19.pin, ...), custom_call_target="tpu_custom_call" | custom-call | tf_op jit(solution)/shard_map/finish/pallas_call | solution.py:651
  (2 shorter events, 0.0 us)
Async XLA Ops:
  0.6 0.7 copy-start
